TPU v7x, 32 devices: a whole 2x2x4 slice. The times are simulated.
32 devices in a mesh: win: 2 (over y), row: 16 (over z, x, core).
Axes of the slice: x: 2, y: 2, z: 4, core: 2. Of those that a mesh axis runs over, the one named last changes fastest.
Arguments:
- image: float32 [3, 2048, 4096], P(None, ('win', 'row')), parts along dimension 1, may hold values from -6 to 6
- grad_x: bfloat16 [3, 2048, 4096], P(None, ('win', 'row')), parts along dimension 1, may hold values from -6 to 6
- grad_y: bfloat16 [3, 2048, 4096], P(None, ('win', 'row')), parts along dimension 1, may hold values from -6 to 6
- classes: int32 [2048, 4096], P(('win', 'row')), parts along dimension 0, may hold values from 0 to 3
- validity: int32 [2, 4], P('win'), parts along dimension 0, may hold values 0 or 1
- owners: int32 [2, 4, 2], P('win'), parts along dimension 0, may hold values from 0 to 1
Outputs:
- solution: float32 [3, 2048, 4096], P(None, ('win', 'row')), parts along dimension 1
There are 2 independent parts, one for each index of `win`. A program takes and returns all parts, laid end to end along the dimension named above; each array names one. Nothing has to cross between parts.
All inputs are finite; a program needn't handle non-finite values.
Results may differ from a plain program's by a relative error of at most 0.0003.
Values may be sent and summed in bfloat16 or wider, within the bound.
No kernel may reach another device: no remote copies, remote signals or barrier semaphores. Data moves between devices by JAX's collectives and lax.ppermute only.
A program may use at most 128 MiB of HBM per device.

v0:
```python
import jax
import jax.numpy as jnp
from jax import lax
from jax.sharding import PartitionSpec as P

TILE_ROWS = 1024
TILE_COLS = 1024
TILES_X = 4
BAND = 48
SWEEPS = 4
WIDTH = 4096


OMEGA = 0.8
SCREEN = 0.25


def passed_along(x, axis, by):
    devices = lax.axis_size(axis)
    pairs = [(i, i + by) for i in range(devices) if 0 <= i + by < devices]
    return lax.ppermute(x, axis, pairs)


def carried_in(x, axis, combine, identity):
    devices, position = (lax.axis_size(axis), lax.axis_index(axis))
    everything = jax.tree.map(lambda part: lax.all_gather(part, axis), x)
    start = jax.tree.map(
        lambda part, zero: jnp.broadcast_to(jnp.asarray(zero, part.dtype), part.shape), x, identity
    )

    def turn(k, before):
        reached = k < position
        new = combine(before, jax.tree.map(lambda part: part[k], everything))
        return jax.tree.map(lambda a, b: jnp.where(reached, a, b), new, before)

    return lax.fori_loop(0, devices, turn, start)


def with_halo(block, sides, width):
    for axis, dim in sides:
        count = lax.axis_size(axis)
        forward = [(i, i + 1) for i in range(count - 1)]
        backward = [(target, source) for source, target in forward]
        low = lax.ppermute(
            lax.slice_in_dim(block, block.shape[dim] - width, None, axis=dim), axis, forward
        )
        high = lax.ppermute(lax.slice_in_dim(block, 0, width, axis=dim), axis, backward)
        block = jnp.concatenate([low, block, high], axis=dim)
    return block


def divergence(horiz_pad, vert_pad):
    horiz_here = horiz_pad[:, 1:, 1:-1]
    horiz_left = horiz_pad[:, 1:, :-2]
    horiz_above = horiz_pad[:, :-1, 1:-1]
    horiz_corner = horiz_pad[:, :-1, :-2]
    vert_here = vert_pad[:, 1:, 1:-1]
    vert_right = vert_pad[:, 1:, 2:]
    vert_left = vert_pad[:, 1:, :-2]
    vert_above = vert_pad[:, :-1, 1:-1]
    diagonal = (
        horiz_here
        + vert_right
        - horiz_corner
        - vert_above
        + vert_left
        - horiz_left
        - vert_above
        + horiz_above
    )
    return horiz_here - horiz_left + vert_here - vert_above + 0.5 * diagonal


def neighbours(padded):
    axial = padded[:, :-2, 1:-1] + padded[:, 2:, 1:-1] + padded[:, 1:-1, :-2] + padded[:, 1:-1, 2:]
    corner = padded[:, :-2, :-2] + padded[:, :-2, 2:] + padded[:, 2:, :-2] + padded[:, 2:, 2:]
    return axial + 0.5 * corner


def relax(row_padded, target, div_term, weights):
    current = row_padded[:, 1:-1, :]
    padded = jnp.pad(row_padded, ((0, 0), (0, 0), (1, 1)))
    return (1.0 - OMEGA) * current + OMEGA * (weights * target + neighbours(padded) - div_term) / (
        weights + 6.0
    )


def join_prefix(earlier, later):
    return (
        earlier[0] + later[0],
        jnp.where(earlier[2] > 0, earlier[1], later[1]),
        jnp.maximum(earlier[2], later[2]),
    )


def per_device(image, grad_x, grad_y, classes, validity, owners):
    band_rows = image.shape[1]
    devices = lax.axis_size("row")
    position = lax.axis_index("row")
    first_row = position * band_rows
    horizontal = grad_x.astype(jnp.float32)
    vertical = grad_y.astype(jnp.float32)
    tile_row = first_row // TILE_ROWS
    own_row = lax.dynamic_index_in_dim(owners, tile_row, 0, keepdims=False)
    lower_mean = passed_along(
        jnp.mean(vertical[:, :BAND, :], axis=1).astype(jnp.bfloat16), "row", -1
    ).astype(jnp.float32)
    upper_mean = jnp.mean(vertical[:, band_rows - 1 - BAND : band_rows - 1, :], axis=1)
    lower_owns = jnp.repeat(own_row[:, 0], TILE_COLS, total_repeat_length=WIDTH)[None] == 1
    at_seam = ((first_row + band_rows) % TILE_ROWS == 0) & (position < devices - 1)
    last_row = jnp.where(at_seam, jnp.where(lower_owns, lower_mean, upper_mean), vertical[:, -1, :])
    vertical = vertical.at[:, -1, :].set(last_row)
    horiz_tiles = horizontal.reshape(3, band_rows, TILES_X, TILE_COLS)
    left_mean = jnp.mean(horiz_tiles[:, :, :-1, TILE_COLS - 1 - BAND : TILE_COLS - 1], axis=3)
    right_mean = jnp.mean(horiz_tiles[:, :, 1:, :BAND], axis=3)
    right_owns = (own_row[:-1, 1] == 1)[None, None, :]
    horiz_tiles = horiz_tiles.at[:, :, :-1, TILE_COLS - 1].set(
        jnp.where(right_owns, right_mean, left_mean)
    )
    horizontal = horiz_tiles.reshape(3, band_rows, WIDTH)
    above_horiz, above_vert = (
        passed_along(horizontal[:, -1:, :].astype(jnp.bfloat16), "row", 1).astype(jnp.float32),
        passed_along(vertical[:, -1:, :].astype(jnp.bfloat16), "row", 1).astype(jnp.float32),
    )
    column_pad = ((0, 0), (0, 0), (1, 1))
    div_term = divergence(
        jnp.pad(jnp.concatenate([above_horiz, horizontal], axis=1), column_pad),
        jnp.pad(jnp.concatenate([above_vert, vertical], axis=1), column_pad),
    )
    mean_vert = jnp.mean(vertical, axis=2)
    mean_image = jnp.mean(image, axis=2)
    running = jnp.cumsum(mean_vert, axis=1) - mean_vert
    totals = jnp.sum(mean_vert, axis=1)
    leading = mean_image[:, 0]
    empty_three = jnp.zeros((3,), jnp.float32)
    before, prior_first, prior_seen = carried_in(
        (totals, leading, jnp.ones((1,), jnp.float32)),
        "row",
        join_prefix,
        (empty_three, empty_three, jnp.zeros((1,), jnp.float32)),
    )
    window_first = jnp.where(prior_seen > 0, prior_first, leading)
    level = before[:, None] + running - mean_image + window_first[:, None]
    target = image + level[:, :, None]
    cover = jnp.repeat(
        lax.dynamic_index_in_dim(validity, tile_row, 0, keepdims=False),
        TILE_COLS,
        total_repeat_length=WIDTH,
    ).astype(jnp.float32)
    weights = cover[None, :] * SCREEN * jnp.exp2(classes.astype(jnp.float32))
    solution = target
    for sweep in range(SWEEPS):
        row_padded = with_halo(solution, (("row", 1),), 1)
        solution = relax(row_padded, target, div_term, weights)
    return solution


def solution(mesh):
    in_specs = (
        P(None, ("win", "row"), None),
        P(None, ("win", "row"), None),
        P(None, ("win", "row"), None),
        P(("win", "row"), None),
        P("win", None),
        P("win", None, None),
    )
    out_specs = P(None, ("win", "row"), None)
    return jax.shard_map(
        per_device, mesh=mesh, in_specs=in_specs, out_specs=out_specs, check_vma=False
    )
```

profile of v0, /device:TPU:0, one launch (start us, length us, event | category | flops | bytes accessed | tf_op | source)
XLA Modules:
  0.0 208.8 jit_solution(10474253459395637235)
XLA Ops:
  1.3 5.1 %reshape.222 = f32[3,64,4,1024]{3,2,1,0:T(4,128)} reshape(bf16[3,64,4096]{2,1,0:T(8,128)(2,1)} %param.19) | data formatting | bytes 4718592 | tf_op jit(solution)/shard_map/reshape | solution.py:113
  6.4 1.8 slice_reduce_fusion.2
  9.7 3.2 %dynamic-slice_select_fusion = f32[3,64,3,1]{3,2,1,0:T(4,128)S(1)} fusion(f32[3,64,4,1024]{3,2,1,0:T(4,128)} %reshape.222, s32[]{:T(128)} %bitcast.19, s32[]{:T(128)} %bitcast.20, f32[3,64,3,1]{3,2,1,0:T(4,128)S(1)} %copy.31, f32[3,64,3,1]{3,2,1,0:T(4,128)S(1)} %copy.32, pred[3]{0:T(512)(128)(4,1)S(1)} %compare_bitcast_fusion, pred[]{:T(512)} %and_reduce_fusion), kind=kLoop, calls=%fused_computation.109 | loop fusion | flops 1152 | bytes 9228 | tf_op jit(solution)/shard_map/select.6
  12.9 34.4 %scatter.9 = f32[3,64,4,1024]{3,2,1,0:T(4,128)} dynamic-update-slice(f32[3,64,4,1024]{3,2,1,0:T(4,128)} %reshape.222, f32[3,64,3,1]{3,2,1,0:T(4,128)S(1)} %dynamic-slice_select_fusion, s32[]{:T(128)} %constant.225.clone.1, s32[]{:T(128)} %constant.225.clone.1, s32[]{:T(128)} %bitcast.19, s32[]{:T(128)} %bitcast.20) | dynamic-update-slice | bytes 4612 | tf_op jit(solution)/shard_map/scatter | solution.py:117
  47.4 3.9 %reshape.220 = f32[3,64,4096]{2,1,0:T(8,128)S(1)} reshape(f32[3,64,4,1024]{3,2,1,0:T(4,128)} %scatter.9) | data formatting | bytes 6291456 | tf_op jit(solution)/shard_map/reshape | solution.py:120
  53.0 2.4 %collective-permute-start.3 = (bf16[3,1,4096]{2,1,0:T(2,128)(2,1)S(1)}, bf16[3,1,4096]{2,1,0:T(2,128)(2,1)S(1)}, u32[]{:S(2)}, u32[]{:S(2)}) collective-permute-start(bf16[3,1,4096]{2,1,0:T(2,128)(2,1)S(1)} %slice.552), channel_id=1, source_target_pairs={{0,1},{1,2},{2,3},{3,4},{4,5},{5,6},{6,7},{7,8},{8,9},{9,10},{10,1... | collective-permute-start | bytes 73736 | tf_op jit(solution)/shard_map/ppermute | solution.py:21
  59.7 2.1 %reduce_sum.67 = f32[3,64]{1,0:T(4,128)S(1)} reduce(f32[3,64,4096]{2,1,0:T(8,128)} %param.18, f32[]{:T(128)} %constant.226.clone.1), dimensions={2}, to_apply=%region_4.6 | reduce | flops 786240 | bytes 3146500 | tf_op jit(solution)/shard_map/reduce_sum | solution.py:131
  62.5 2.5 %fusion.46 = f32[4096]{0:T(1024)S(1)} fusion(pred[4096]{0:T(1024)(128)(4,1)S(1)} %copy-done.9, pred[4096]{0:T(1024)(128)(4,1)S(1)} %copy-done.8, pred[4096]{0:T(1024)(128)(4,1)S(1)} %copy-done.7, s32[]{:T(128)} %bitcast.15, s32[]{:T(128)} %bitcast.14, s32[]{:T(128)} %bitcast.13, s32[]{:T(128)} %bitcast.12), kind=kLoop, calls=%fused_computation.117 | loop fusion | flops 20480 | bytes 28688 | tf_op jit(solution)/shard_map/mul | solution.py:150
  65.0 2.8 %broadcast_add_fusion.1 = (f32[64,4096]{1,0:T(8,128)}, f32[64,4096]{1,0:T(8,128)}) fusion(s32[64,4096]{1,0:T(8,128)} %param.21, f32[4096]{0:T(1024)S(1)} %fusion.46), kind=kLoop, calls=%fused_computation.106 | loop fusion | flops 1048576 | bytes 3162112 | tf_op jit(solution)/shard_map/add | solution.py:84
  67.8 2.6 %select_compare_fusion = pred[4096]{0:T(1024)(128)(4,1)S(1)} fusion(pred[4096]{0:T(1024)(128)(4,1)S(1)} %copy-done.9, pred[4096]{0:T(1024)(128)(4,1)S(1)} %copy-done.8, pred[4096]{0:T(1024)(128)(4,1)S(1)} %copy-done.7, s32[]{:T(128)} %bitcast.5, s32[]{:T(128)} %bitcast.4, s32[]{:T(128)} %bitcast.3, s32[]{:T(128)} %bitcast.2), kind=kLoop, calls=%fused_computation.118 | loop fusion | flops 16384 | bytes 16400 | tf_op jit(solution)/shard_map/eq | solution.py:109
  74.9 35.7 %all-reduce.9 = (f32[48]{0:T(128)S(1)}, f32[48]{0:T(128)S(1)}, f32[16]{0:T(128)S(1)}) all-reduce(f32[48]{0:T(128)S(1)} %dynamic-update-slice.10, f32[48]{0:T(128)S(1)} %dynamic-update-slice.11, f32[16]{0:T(128)S(1)} %dynamic-update-slice.12), channel_id=2, replica_groups=mesh['win'=2,'row'=16] {'row'}, use_global_device_ids=true, to_apply=%add.6 | all-reduce | flops 112 | bytes 896
  110.8 19.4 %while.22 = (s32[]{:T(128)}, f32[3]{0:T(128)S(1)}, f32[3]{0:T(128)S(1)}, f32[1]{0:T(128)}, s32[]{:T(128)}, /*index=5*/f32[16,3]{1,0:T(8,128)S(1)}, f32[16,3]{1,0...) while((s32[]{:T(128)}, f32[3]{0:T(128)S(1)}, f32[3]{0:T(128)S(1)}, ...), condition=%wide.region_6.8_spmd.clone, body=%wide.region_5.7_spmd.clone.sunk | while | flops 25 | bytes 260 | solution.py:36
  131.9 2.4 %broadcast_add_fusion = f32[3,64,4096]{2,1,0:T(8,128)S(1)} fusion(f32[3,64,4096]{2,1,0:T(8,128)} %param.18, f32[3,64]{1,0:T(4,128)S(1)} %subtract_add_fusion), kind=kLoop, calls=%fused_computation.104 | loop fusion | flops 786432 | bytes 6292224 | tf_op jit(solution)/shard_map/add | solution.py:144
  137.3 2.3 %pad_maximum_fusion = f32[3,65,4096]{2,1,0:T(8,128)} fusion(f32[3,1,4096]{2,1,0:T(1,128)S(1)} %convert_element_type.42, f32[3,64,4096]{2,1,0:T(8,128)S(1)} %copy-done.3), kind=kLoop, calls=%fused_computation.13 | loop fusion | flops 798720 | bytes 6389760 | tf_op jit(solution)/shard_map/concatenate | solution.py:127
  139.7 2.3 %pad_maximum_fusion.1 = f32[3,65,4096]{2,1,0:T(8,128)} fusion(f32[3,1,4096]{2,1,0:T(1,128)S(1)} %convert_element_type.45, f32[3,64,4096]{2,1,0:T(8,128)S(1)} %scatter.6), kind=kLoop, calls=%fused_computation.15 | loop fusion | flops 798720 | bytes 6389760 | tf_op jit(solution)/shard_map/concatenate | solution.py:128
  143.2 10.5 %fusion.44 = (f32[3,64,4096]{2,1,0:T(8,128)S(1)}, f32[3,64,4096]{2,1,0:T(8,128)S(1)}) fusion(f32[3,66,4098]{2,1,0:T(8,128)S(1)} %select_maximum_fusion.6, f32[3,1,4096]{2,1,0:T(1,128)S(1)} %collective-permute-done.2, f32[3,64,4096]{2,1,0:T(8,128)S(1)} %broadcast_add_fusion, f32[3,1,4096]{2,1,0:T(1,128)S(1)} %collective-permute-done.1, ...), kind=kLoop, calls=%fused_computation.94 | loop fusion | flops 24379392 | bytes 43286528 | tf_op jit(solution)/shard_map/add | solution.py:83
  153.8 3.0 %collective-permute-start.5 = (f32[3,1,4096]{2,1,0:T(1,128)S(1)}, f32[3,1,4096]{2,1,0:T(1,128)S(1)}, u32[]{:S(2)}, u32[]{:S(2)}) collective-permute-start(f32[3,1,4096]{2,1,0:T(1,128)S(1)} %get-tuple-element.254), channel_id=1, source_target_pairs={{0,1},{1,2},{2,3},{3,4},{4,5},{5,6},{6,7},{7,8},{8,9},{9,10},{10,1... | collective-permute-start | bytes 147464 | tf_op jit(solution)/shard_map/ppermute | solution.py:44
  161.5 7.9 %fusion.36 = f32[3,64,4096]{2,1,0:T(8,128)} fusion(f32[3,64,4096]{2,1,0:T(8,128)S(1)} %get-tuple-element.245, f32[3,66,4098]{2,1,0:T(8,128)S(1)} %select_maximum_fusion.4, f32[3,1,4096]{2,1,0:T(1,128)S(1)} %collective-permute-done.6, f32[3,64,4096]{2,1,0:T(8,128)} %copy-done.1, f32[3,1,4096]{2,1,0:T(1,128)S(1)} %collective-permute-done.5, ...), kind=kLoop, calls=%fused_computation.79 | loop fusion | flops 14155776 | bytes 33653504 | tf_op jit(solution)/shard_map/add | solution.py:83
  170.7 4.2 %collective-permute-start.7 = (f32[3,1,4096]{2,1,0:T(1,128)S(1)}, f32[3,1,4096]{2,1,0:T(1,128)S(1)}, u32[]{:S(2)}, u32[]{:S(2)}) collective-permute-start(f32[3,1,4096]{2,1,0:T(1,128)S(1)} %get-tuple-element.252), channel_id=1, source_target_pairs={{0,1},{1,2},{2,3},{3,4},{4,5},{5,6},{6,7},{7,8},{8,9},{9,10},{10,1... | collective-permute-start | bytes 147464 | tf_op jit(solution)/shard_map/ppermute | solution.py:44
  178.0 3.1 %select_maximum_fusion.2 = f32[3,66,4098]{2,1,0:T(8,128)S(1)} fusion(f32[3,1,4096]{2,1,0:T(1,128)S(1)} %collective-permute-done.8, f32[3,64,4096]{2,1,0:T(8,128)} %fusion.36, f32[3,1,4096]{2,1,0:T(1,128)S(1)} %collective-permute-done.7), kind=kLoop, calls=%fused_computation.18 | loop fusion | flops 6491232 | bytes 6489648 | tf_op jit(solution)/shard_map/concatenate | solution.py:48
  181.1 8.1 %fusion.28 = f32[3,64,4096]{2,1,0:T(8,128)} fusion(f32[3,64,4096]{2,1,0:T(8,128)S(1)} %get-tuple-element.245, f32[3,66,4098]{2,1,0:T(8,128)S(1)} %select_maximum_fusion.2, f32[3,1,4096]{2,1,0:T(1,128)S(1)} %collective-permute-done.8, f32[3,64,4096]{2,1,0:T(8,128)} %fusion.36, f32[3,1,4096]{2,1,0:T(1,128)S(1)} %collective-permute-done.7, ...), kind=kLoop, calls=%fused_computation.64 | loop fusion | flops 14155776 | bytes 33653504 | tf_op jit(solution)/shard_map/add | solution.py:83
  190.4 4.2 %collective-permute-start.9 = (f32[3,1,4096]{2,1,0:T(1,128)S(1)}, f32[3,1,4096]{2,1,0:T(1,128)S(1)}, u32[]{:S(2)}, u32[]{:S(2)}) collective-permute-start(f32[3,1,4096]{2,1,0:T(1,128)S(1)} %get-tuple-element.250), channel_id=1, source_target_pairs={{0,1},{1,2},{2,3},{3,4},{4,5},{5,6},{6,7},{7,8},{8,9},{9,10},{10,1... | collective-permute-start | bytes 147464 | tf_op jit(solution)/shard_map/ppermute | solution.py:44
  197.8 3.1 %select_maximum_fusion = f32[3,66,4098]{2,1,0:T(8,128)S(1)} fusion(f32[3,1,4096]{2,1,0:T(1,128)S(1)} %collective-permute-done.10, f32[3,64,4096]{2,1,0:T(8,128)} %fusion.28, f32[3,1,4096]{2,1,0:T(1,128)S(1)} %collective-permute-done.9), kind=kLoop, calls=%fused_computation.16 | loop fusion | flops 6491232 | bytes 6489648 | tf_op jit(solution)/shard_map/concatenate | solution.py:48
  200.9 7.9 %fusion.20 = f32[3,64,4096]{2,1,0:T(8,128)} fusion(f32[3,64,4096]{2,1,0:T(8,128)S(1)} %get-tuple-element.245, f32[3,66,4098]{2,1,0:T(8,128)S(1)} %select_maximum_fusion, f32[3,1,4096]{2,1,0:T(1,128)S(1)} %collective-permute-done.10, f32[3,64,4096]{2,1,0:T(8,128)} %fusion.28, f32[3,1,4096]{2,1,0:T(1,128)S(1)} %collective-permute-done.9, ...), kind=kLoop, calls=%fused_computation.49 | loop fusion | flops 14155776 | bytes 33653504 | tf_op jit(solution)/shard_map/add | solution.py:83
  (126 shorter events, 42.3 us)
Async XLA Ops:
  1.3 7.7 %copy-start.11 = (s32[4]{0:T(128)S(1)}, s32[4]{0:T(128)}, u32[]{:S(2)}) copy-start(s32[4]{0:T(128)} %constant.244.clone.1) | copy-start | bytes 52
  51.3 1.7 copy-start.2
  53.0 84.2 %collective-permute-start.3 = (bf16[3,1,4096]{2,1,0:T(2,128)(2,1)S(1)}, bf16[3,1,4096]{2,1,0:T(2,128)(2,1)S(1)}, u32[]{:S(2)}, u32[]{:S(2)}) collective-permute-start(bf16[3,1,4096]{2,1,0:T(2,128)(2,1)S(1)} %slice.552), channel_id=1, source_target_pairs={{0,1},{1,2},{2,3},{3,4},{4,5},{5,6},{6,7},{7,8},{8,9},{9,10},{10,1... | collective-permute-start | bytes 73736 | tf_op jit(solution)/shard_map/ppermute | solution.py:21
  57.1 1.9 copy-start.12
  57.2 4.7 %copy-start.10 = (s32[1,4]{1,0:T(1,128)S(1)}, s32[1,4]{1,0:T(1,128)}, u32[]{:S(2)}) copy-start(s32[1,4]{1,0:T(1,128)} %param.22) | copy-start | bytes 52
  57.2 5.3 %copy-start.7 = (pred[4096]{0:T(1024)(128)(4,1)S(1)}, pred[4096]{0:T(1024)(128)(4,1)}, u32[]{:S(2)}) copy-start(pred[4096]{0:T(1024)(128)(4,1)} %constant.303) | copy-start | bytes 12292
  57.2 5.3 %copy-start.8 = (pred[4096]{0:T(1024)(128)(4,1)S(1)}, pred[4096]{0:T(1024)(128)(4,1)}, u32[]{:S(2)}) copy-start(pred[4096]{0:T(1024)(128)(4,1)} %constant.302) | copy-start | bytes 12292
  57.2 5.3 %copy-start.9 = (pred[4096]{0:T(1024)(128)(4,1)S(1)}, pred[4096]{0:T(1024)(128)(4,1)}, u32[]{:S(2)}) copy-start(pred[4096]{0:T(1024)(128)(4,1)} %constant.301) | copy-start | bytes 12292
  57.7 16.0 %collective-permute-start = (bf16[3,4096]{1,0:T(4,128)(2,1)S(1)}, bf16[3,4096]{1,0:T(4,128)(2,1)S(1)}, u32[]{:S(2)}, u32[]{:S(2)}) collective-permute-start(bf16[3,4096]{1,0:T(4,128)(2,1)S(1)} %multiply_convert_fusion), channel_id=1, source_target_pairs={{1,0},{2,1},{3,2},{4,3},{5,4},{6,5},{7,6},{8,7},{9,8},{10,9},{11,1... | collective-permute-start | bytes 73736 | tf_op jit(solution)/shard_map/ppermute | solution.py:21
  59.7 11.8 %copy-start.13 = (u32[32]{0:T(128)S(1)}, u32[32]{0:T(128)}, u32[]{:S(2)}) copy-start(u32[32]{0:T(128)} %constant.284) | copy-start | bytes 388
  130.3 9.3 %collective-permute-start.4 = (bf16[3,1,4096]{2,1,0:T(2,128)(2,1)S(1)}, bf16[3,1,4096]{2,1,0:T(2,128)(2,1)S(1)}, u32[]{:S(2)}, u32[]{:S(2)}) collective-permute-start(bf16[3,1,4096]{2,1,0:T(2,128)(2,1)S(1)} %copy.33), channel_id=1, source_target_pairs={{0,1},{1,2},{2,3},{3,4},{4,5},{5,6},{6,7},{7,8},{8,9},{9,10},{10,1... | collective-permute-start | bytes 73736 | tf_op jit(solution)/shard_map/ppermute | solution.py:21
  131.9 5.3 %copy-start.3 = (f32[3,64,4096]{2,1,0:T(8,128)S(1)}, f32[3,64,4096]{2,1,0:T(8,128)}, u32[]{:S(2)}) copy-start(f32[3,64,4096]{2,1,0:T(8,128)} %copy-done.2) | copy-start | bytes 9437188
  134.4 7.5 %collective-permute-start.1 = (f32[3,1,4096]{2,1,0:T(1,128)S(1)}, f32[3,1,4096]{2,1,0:T(1,128)S(1)}, u32[]{:S(2)}, u32[]{:S(2)}) collective-permute-start(f32[3,1,4096]{2,1,0:T(1,128)S(1)} %get-tuple-element.256), channel_id=1, source_target_pairs={{0,1},{1,2},{2,3},{3,4},{4,5},{5,6},{6,7},{7,8},{8,9},{9,10},{10,1... | collective-permute-start | bytes 147464 | tf_op jit(solution)/shard_map/ppermute | solution.py:44
  135.7 6.2 %collective-permute-start.2 = (f32[3,1,4096]{2,1,0:T(1,128)S(1)}, f32[3,1,4096]{2,1,0:T(1,128)S(1)}, u32[]{:S(2)}, u32[]{:S(2)}) collective-permute-start(f32[3,1,4096]{2,1,0:T(1,128)S(1)} %get-tuple-element.257), channel_id=1, source_target_pairs={{1,0},{2,1},{3,2},{4,3},{5,4},{6,5},{7,6},{8,7},{9,8},{10,9},{11,1... | collective-permute-start | bytes 147464 | tf_op jit(solution)/shard_map/ppermute | solution.py:47
  153.7 7.8 %copy-start.1 = (f32[3,64,4096]{2,1,0:T(8,128)}, f32[3,64,4096]{2,1,0:T(8,128)S(1)}, u32[]{:S(2)}) copy-start(f32[3,64,4096]{2,1,0:T(8,128)S(1)} %get-tuple-element.244) | copy-start | bytes 9437188
  153.8 4.6 %collective-permute-start.5 = (f32[3,1,4096]{2,1,0:T(1,128)S(1)}, f32[3,1,4096]{2,1,0:T(1,128)S(1)}, u32[]{:S(2)}, u32[]{:S(2)}) collective-permute-start(f32[3,1,4096]{2,1,0:T(1,128)S(1)} %get-tuple-element.254), channel_id=1, source_target_pairs={{0,1},{1,2},{2,3},{3,4},{4,5},{5,6},{6,7},{7,8},{8,9},{9,10},{10,1... | collective-permute-start | bytes 147464 | tf_op jit(solution)/shard_map/ppermute | solution.py:44
  156.8 4.7 %copy-start = (f32[3,64,4096]{2,1,0:T(8,128)S(1)}, f32[3,64,4096]{2,1,0:T(8,128)}, u32[]{:S(2)}) copy-start(f32[3,64,4096]{2,1,0:T(8,128)} %param.18) | copy-start | bytes 9437188
  156.8 4.7 %copy-start.5 = (f32[64,4096]{1,0:T(8,128)S(1)}, f32[64,4096]{1,0:T(8,128)}, u32[]{:S(2)}) copy-start(f32[64,4096]{1,0:T(8,128)} %get-tuple-element.246) | copy-start | bytes 3145732
  156.9 4.7 %copy-start.6 = (f32[64,4096]{1,0:T(8,128)S(1)}, f32[64,4096]{1,0:T(8,128)}, u32[]{:S(2)}) copy-start(f32[64,4096]{1,0:T(8,128)} %get-tuple-element.247) | copy-start | bytes 3145732
  156.9 3.4 %collective-permute-start.6 = (f32[3,1,4096]{2,1,0:T(1,128)S(1)}, f32[3,1,4096]{2,1,0:T(1,128)S(1)}, u32[]{:S(2)}, u32[]{:S(2)}) collective-permute-start(f32[3,1,4096]{2,1,0:T(1,128)S(1)} %get-tuple-element.255), channel_id=1, source_target_pairs={{1,0},{2,1},{3,2},{4,3},{5,4},{6,5},{7,6},{8,7},{9,8},{10,9},{11,1... | collective-permute-start | bytes 147464 | tf_op jit(solution)/shard_map/ppermute | solution.py:47
  170.7 5.5 %collective-permute-start.7 = (f32[3,1,4096]{2,1,0:T(1,128)S(1)}, f32[3,1,4096]{2,1,0:T(1,128)S(1)}, u32[]{:S(2)}, u32[]{:S(2)}) collective-permute-start(f32[3,1,4096]{2,1,0:T(1,128)S(1)} %get-tuple-element.252), channel_id=1, source_target_pairs={{0,1},{1,2},{2,3},{3,4},{4,5},{5,6},{6,7},{7,8},{8,9},{9,10},{10,1... | collective-permute-start | bytes 147464 | tf_op jit(solution)/shard_map/ppermute | solution.py:44
  174.9 3.1 %collective-permute-start.8 = (f32[3,1,4096]{2,1,0:T(1,128)S(1)}, f32[3,1,4096]{2,1,0:T(1,128)S(1)}, u32[]{:S(2)}, u32[]{:S(2)}) collective-permute-start(f32[3,1,4096]{2,1,0:T(1,128)S(1)} %get-tuple-element.253), channel_id=1, source_target_pairs={{1,0},{2,1},{3,2},{4,3},{5,4},{6,5},{7,6},{8,7},{9,8},{10,9},{11,1... | collective-permute-start | bytes 147464 | tf_op jit(solution)/shard_map/ppermute | solution.py:47
  190.4 5.7 %collective-permute-start.9 = (f32[3,1,4096]{2,1,0:T(1,128)S(1)}, f32[3,1,4096]{2,1,0:T(1,128)S(1)}, u32[]{:S(2)}, u32[]{:S(2)}) collective-permute-start(f32[3,1,4096]{2,1,0:T(1,128)S(1)} %get-tuple-element.250), channel_id=1, source_target_pairs={{0,1},{1,2},{2,3},{3,4},{4,5},{5,6},{6,7},{7,8},{8,9},{9,10},{10,1... | collective-permute-start | bytes 147464 | tf_op jit(solution)/shard_map/ppermute | solution.py:44
  194.6 3.1 %collective-permute-start.10 = (f32[3,1,4096]{2,1,0:T(1,128)S(1)}, f32[3,1,4096]{2,1,0:T(1,128)S(1)}, u32[]{:S(2)}, u32[]{:S(2)}) collective-permute-start(f32[3,1,4096]{2,1,0:T(1,128)S(1)} %get-tuple-element.251), channel_id=1, source_target_pairs={{1,0},{2,1},{3,2},{4,3},{5,4},{6,5},{7,6},{8,7},{9,8},{10,9},{11,1... | collective-permute-start | bytes 147464 | tf_op jit(solution)/shard_map/ppermute | solution.py:47
  (1 other events, 1.3 us)
where the time goes:
time: 212 us; the launch traced here: 209 us
  other arithmetic  70.1 us (33%)
  local copies, waits for them, and re-layouts  63.3 us (30%)
  blocking collectives  35.7 us (17%)
  starting transfers between devices  23.5 us (11%)
  loops' own time  9.62 us (5%)
  waiting for transfers between devices  5.24 us (2%)
    unnamed x1, blocking collectives  35.7 us
    scatter x1, local copies, waits for them, and re-layouts, per_device(): horiz_tiles.at[:, :, :-1, TILE_COLS - 1]  34.4 us
    add x4, other arithmetic, relax(): (1.0 - OMEGA) * current  34.4 us
    ppermute x4, starting transfers between devices, with_halo(): lax.ppermute(lax.slice_in_dim(block, block.shape[dim] - width, None, axis...  12.7 us
    another operation x1, loops' own time, carried_in(): return lax.fori_loop(0, devices, turn, start)  9.62 us
    dynamic_slice x16, local copies, waits for them, and re-layouts, turn(): new = combine(before, jax.tree.map(lambda part: part[k], everything))  9.46 us
    concatenate x4, other arithmetic, with_halo(): block = jnp.concatenate([low, block, high], axis=dim)  8.71 us
    ppermute x4, starting transfers between devices, with_halo(): lax.ppermute(lax.slice_in_dim(block, 0, width, axis=dim), axis, backward)  5.83 us
  transfers between devices with their start and end apart: 11, of which 3 were waited for; matrix products, arithmetic and copies ran while one was open for 17% of the time, Pallas kernels for 0%

commit v1 on v0

v1 whole, which is shorter than its diff:
```python
import jax
import jax.numpy as jnp
from jax import lax
from jax.experimental import pallas as pl
from jax.experimental.pallas import tpu as pltpu
from jax.sharding import PartitionSpec as P

TILE_ROWS = 1024
TILE_COLS = 1024
BAND = 48
SWEEPS = 4
OMEGA = 0.8
SCREEN = 0.25

LANES = 128
HALO = SWEEPS
TOP = 8
FIRST = TOP + HALO
f32 = jnp.float32
bf16 = jnp.bfloat16


def lane_tile(j):
    return slice(j * LANES, (j + 1) * LANES)


def sublane_ids():
    return lax.broadcasted_iota(jnp.int32, (8, LANES), 0)


def lane_ids():
    return lax.broadcasted_iota(jnp.int32, (8, LANES), 1)


def pack_kernel(image, gx, gy, classes, gy_all, to_a, to_b, sums, img_e, gx_e, gy_e, cls_e, sem):
    channels, rows, width = image.shape
    tiles = width // LANES
    position = lax.axis_index("row")
    even = position % 2 == 0
    copies = []
    for side, start in enumerate((0, rows - 8)):
        window = pl.ds(start, 8)
        for n, (src, dst) in enumerate(((image, img_e), (gx, gx_e), (gy, gy_e))):
            copies.append(pltpu.make_async_copy(src.at[:, window, :], dst.at[side], sem.at[side, n]))
        copies.append(pltpu.make_async_copy(classes.at[window, :], cls_e.at[side], sem.at[side, 3]))
    for copy in copies:
        copy.start()
    low_half = sublane_ids() < 4
    for k in range(channels):
        total = jnp.zeros((8, LANES), f32)

        def add_rows(g, acc):
            for j in range(tiles):
                x = gy_all[k, pl.ds(g * 16, 16), lane_tile(j)].astype(f32)
                acc = acc + (x[:8] + x[8:])
            return acc

        total = lax.fori_loop(0, rows // 16, add_rows, total)
        total = jnp.sum(jnp.sum(total, axis=1, keepdims=True), axis=0, keepdims=True) / width
        sums[k : k + 1, :] = jnp.broadcast_to(total, (1, LANES))
    for copy in copies:
        copy.wait()
    for k in range(channels):
        lead = jnp.zeros((8, LANES), f32)
        for j in range(tiles):
            lead = lead + img_e[0, k, :, lane_tile(j)]
        lead = jnp.sum(lead[0:1, :], axis=1, keepdims=True) / width
        lead = jnp.where(position == 0, lead, 0.0)
        sums[channels + k : channels + k + 1, :] = jnp.broadcast_to(lead, (1, LANES))
    if 2 * channels < 8:
        sums[2 * channels :, :] = jnp.zeros((8 - 2 * channels, LANES), f32)

    def joined(side, first, second):
        if side == 0:
            return jnp.where(low_half, first, pltpu.roll(second, 4, 0))
        return jnp.where(low_half, pltpu.roll(first, 4, 0), second)

    def fill(side, out):
        def one(j):
            at = pl.ds(pl.multiple_of(j * LANES, LANES), LANES)
            for k in range(channels):
                x = img_e[side, k, :, at]
                high = x.astype(bf16).astype(f32)
                out[2 * k, :, at] = joined(side, high, x - high).astype(bf16)
                out[2 * k + 1, :, at] = joined(
                    side, gx_e[side, k, :, at].astype(f32), gy_e[side, k, :, at].astype(f32)
                ).astype(bf16)
            c = cls_e[side, :, at].astype(f32)
            out[2 * channels, :, at] = joined(side, c, c).astype(bf16)

        def step(j, carry):
            one(j)
            return carry

        lax.fori_loop(0, tiles, step, 0, unroll=4)

    @pl.when(even)
    def _():
        fill(1, to_a)
        fill(0, to_b)

    @pl.when(jnp.logical_not(even))
    def _():
        fill(0, to_a)
        fill(1, to_b)


def pack(image, gx, gy, classes):
    channels, rows, width = image.shape
    hbm = pl.BlockSpec(memory_space=pl.ANY)
    edge = jax.ShapeDtypeStruct((2 * channels + 1, 8, width), bf16)
    return pl.pallas_call(
        pack_kernel,
        out_shape=(edge, edge, jax.ShapeDtypeStruct((8, LANES), f32)),
        in_specs=[hbm, hbm, hbm, hbm, pl.BlockSpec(memory_space=pltpu.VMEM)],
        out_specs=[pl.BlockSpec(memory_space=pltpu.VMEM)] * 3,
        scratch_shapes=[
            pltpu.VMEM((2, channels, 8, width), f32),
            pltpu.VMEM((2, channels, 8, width), bf16),
            pltpu.VMEM((2, channels, 8, width), bf16),
            pltpu.VMEM((2, 8, width), jnp.int32),
            pltpu.SemaphoreType.DMA((2, 4)),
        ],
        name="pack",
    )(image, gx, gy, classes, gy)


def main_kernel(
    validity, owners, offset, from_a, from_b, image, gx, gy, classes, out,
    halo, q_s, qw_s, x_s, y_s, s_s, t_s, b_s, row_y, row_i, level, sem,
):
    channels = pl.num_programs(0)
    k = pl.program_id(0)
    _, rows, width = image.shape
    tiles = width // LANES
    per_tile = TILE_COLS // LANES
    groups = (rows + 2 * HALO) // 8
    n_classes = 6
    position = lax.axis_index("row")
    last = lax.axis_size("row") - 1
    even = position % 2 == 0
    above = position > 0
    below = position < last
    tile_row = position * rows // TILE_ROWS
    lanes = lane_ids()
    first_lane = lanes == 0
    last_lane = lanes == LANES - 1

    @pl.when(k == 0)
    def _():
        @pl.when(even)
        def _():
            pltpu.make_async_copy(from_b, halo.at[0], sem.at[0]).start()
            pltpu.make_async_copy(from_a, halo.at[1], sem.at[1]).start()

        @pl.when(jnp.logical_not(even))
        def _():
            pltpu.make_async_copy(from_a, halo.at[0], sem.at[0]).start()
            pltpu.make_async_copy(from_b, halo.at[1], sem.at[1]).start()

        for ref in (q_s, qw_s, x_s, y_s, s_s, t_s, b_s):
            for j in range(tiles):
                ref[j, 0:8, :] = jnp.zeros((8, LANES), f32)
                ref[j, TOP + 8 * groups : TOP + 8 * groups + 8, :] = jnp.zeros((8, LANES), f32)

    def factors(c, cover):
        w = cover * SCREEN * jnp.exp2(c)
        q = OMEGA / (w + 6.0)
        return q, q * w

    @pl.when(k == 0)
    def _():
        covers = [validity[tile_row, b].astype(f32) for b in range(width // TILE_COLS)]

        def natural(g, carry):
            at = pl.multiple_of(g * 8, 8)
            for j in range(tiles):
                q, qw = factors(classes[pl.ds(at, 8), lane_tile(j)].astype(f32), covers[j // per_tile])
                q_s[j, pl.ds(FIRST + at, 8), :] = q
                qw_s[j, pl.ds(FIRST + at, 8), :] = qw
            return carry

        lax.fori_loop(0, rows // 8, natural, 0)
        pltpu.make_async_copy(from_a, halo.at[0], sem.at[0]).wait()
        pltpu.make_async_copy(from_a, halo.at[1], sem.at[1]).wait()
        for side, there, at in ((0, above, TOP), (1, below, FIRST + rows)):
            beyond = jnp.where(
                side == 0,
                jnp.maximum(position * rows - 1, 0) // TILE_ROWS,
                jnp.minimum((position + 1) * rows, (last + 1) * rows - 1) // TILE_ROWS,
            )
            for j in range(tiles):
                cover = validity[beyond, j // per_tile].astype(f32)
                q, qw = factors(halo[side, n_classes, :, lane_tile(j)].astype(f32), cover)
                q_s[j, at : at + HALO, :] = jnp.where(there, q, 0.0)[:HALO]
                qw_s[j, at : at + HALO, :] = jnp.where(there, qw, 0.0)[:HALO]

    def unpack(g, carry):
        at = pl.multiple_of(g * 16, 16)
        sum_y = jnp.zeros((16, LANES), f32)
        sum_i = jnp.zeros((16, LANES), f32)
        for j in range(tiles):
            here = pl.ds(FIRST + at, 16)
            x_s[j, here, :] = gx[0, pl.ds(at, 16), lane_tile(j)].astype(f32)
            y = gy[0, pl.ds(at, 16), lane_tile(j)].astype(f32)
            y_s[j, here, :] = y
            i = image[0, pl.ds(at, 16), lane_tile(j)]
            s_s[j, here, :] = i
            sum_y = sum_y + y
            sum_i = sum_i + i
        row_y[pl.ds(FIRST + at, 16), :] = sum_y
        row_i[pl.ds(FIRST + at, 16), :] = sum_i
        return carry

    lax.fori_loop(0, rows // 16, unpack, 0)
    for side, at in ((0, TOP), (1, FIRST + rows)):
        sum_y = jnp.zeros((8, LANES), f32)
        sum_i = jnp.zeros((8, LANES), f32)
        for j in range(tiles):
            v = halo[side, 2 * k, :, lane_tile(j)].astype(f32)
            i = v + pltpu.roll(v, 4, 0)
            s_s[j, at : at + HALO, :] = i[:HALO]
            g = halo[side, 2 * k + 1, :, lane_tile(j)].astype(f32)
            y = pltpu.roll(g, 4, 0)
            x_s[j, at : at + HALO, :] = g[:HALO]
            y_s[j, at : at + HALO, :] = y[:HALO]
            sum_y = sum_y + y
            sum_i = sum_i + i
        row_y[at : at + HALO, :] = sum_y[:HALO]
        row_i[at : at + HALO, :] = sum_i[:HALO]

    for b in range(width // TILE_COLS - 1):
        j = (b + 1) * per_tile - 1
        for g in range(groups):
            at = TOP + 8 * g
            if g == 0:
                other = jnp.maximum(position * rows - 1, 0) // TILE_ROWS
            elif g == groups - 1:
                other = jnp.minimum((position + 1) * rows, (last + 1) * rows - 1) // TILE_ROWS
            else:
                other = tile_row
            left = x_s[j, at : at + 8, :]
            right = x_s[j + 1, at : at + 8, :]
            right_sum = jnp.sum(jnp.where(lanes < BAND, right, 0.0), axis=1, keepdims=True)
            left_sum = jnp.sum(
                jnp.where((lanes >= LANES - 1 - BAND) & (lanes < LANES - 1), left, 0.0), axis=1, keepdims=True
            )
            own = jnp.where(owners[tile_row, b, 1] == 1, right_sum, left_sum)
            if g in (0, groups - 1):
                far = jnp.where(owners[other, b, 1] == 1, right_sum, left_sum)
                half = sublane_ids() < HALO
                own = jnp.where(half == (g == 0), far, own)
            x_s[j, at : at + 8, :] = jnp.where(last_lane, own / BAND, left)

    r = lax.broadcasted_iota(jnp.int32, (8 * groups, 8 * groups), 0)
    c = lax.broadcasted_iota(jnp.int32, (8 * groups, 8 * groups), 1)
    reach = jnp.where((c < r) & (c >= HALO), 1.0, jnp.where((c >= r) & (c < HALO), -1.0, 0.0))
    span = slice(TOP, TOP + 8 * groups)
    climbed = jnp.dot(reach, row_y[span, :], precision=lax.Precision.HIGHEST, preferred_element_type=f32)
    lv = jnp.sum(climbed - row_i[span, :], axis=1, keepdims=True) / width
    lv = jnp.broadcast_to(lv, (8 * groups, LANES)) + (
        offset[pl.ds(k, 1), :] + offset[pl.ds(k + channels, 1), :]
    )
    row = lax.broadcasted_iota(jnp.int32, (8 * groups, LANES), 0) - HALO
    inside = ((row >= 0) | above) & ((row < rows) | below)
    level[...] = jnp.where(inside, lv, 0.0)

    def shifted(prev, rots, nxt, j):
        pass

    def terms(g, carry):
        at = pl.multiple_of(TOP + g * 8, 8)
        lv = level[pl.ds(pl.multiple_of(g * 8, 8), 8), :]
        fs, ys = [], []
        left_t = right_y = None

        def load(j):
            x = x_s[j, pl.ds(at, 8), :]
            xu = x_s[j, pl.ds(at - 1, 8), :]
            y = y_s[j, pl.ds(at, 8), :]
            yu = y_s[j, pl.ds(at - 1, 8), :]
            f = 3.0 * x + xu
            base = f + 2.0 * (y - 2.0 * yu)
            return base, pltpu.roll(y - f, 1, 1), pltpu.roll(y, LANES - 1, 1)

        zero = jnp.zeros((8, LANES), f32)
        prev_rot = zero
        cur = load(0)
        for j in range(tiles):
            nxt = load(j + 1) if j + 1 < tiles else (None, None, zero)
            base, rot_l, rot_r = cur
            twice = base + jnp.where(first_lane, prev_rot, rot_l) + jnp.where(last_lane, nxt[2], rot_r)
            q = q_s[j, pl.ds(at, 8), :]
            qw = qw_s[j, pl.ds(at, 8), :]
            t = s_s[j, pl.ds(at, 8), :] + lv
            s_s[j, pl.ds(at, 8), :] = t
            b_s[j, pl.ds(at, 8), :] = qw * t - (0.5 * q) * twice
            prev_rot = rot_l
            cur = nxt
        return carry

    lax.fori_loop(0, groups, terms, 0)

    def sweep(src, write, count, start):
        def body(g, carry):
            at = start + g * 8

            def load(j):
                s = src[j, pl.ds(at, 8), :]
                u = src[j, pl.ds(at - 1, 8), :] + src[j, pl.ds(at + 1, 8), :]
                a = s + 0.5 * u
                return s, u, pltpu.roll(a, 1, 1), pltpu.roll(a, LANES - 1, 1)

            zero = jnp.zeros((8, LANES), f32)
            prev_rot = zero
            cur = load(0)
            for j in range(tiles):
                nxt = load(j + 1) if j + 1 < tiles else (None, None, None, zero)
                s, u, rot_l, rot_r = cur
                n = u + jnp.where(first_lane, prev_rot, rot_l) + jnp.where(last_lane, nxt[3], rot_r)
                new = (1.0 - OMEGA) * s + (q_s[j, pl.ds(at, 8), :] * n + b_s[j, pl.ds(at, 8), :])
                write(g, j, at, new)
                prev_rot = rot_l
                cur = nxt
            return carry

        lax.fori_loop(0, count, body, 0)

    def into(dst):
        def write(g, j, at, v):
            dst[j, pl.ds(at, 8), :] = v

        return write

    def finish(g, j, at, v):
        out[0, pl.ds(pl.multiple_of(g * 8, 8), 8), lane_tile(j)] = v

    src, dst = s_s, t_s
    for _ in range(SWEEPS - 1):
        sweep(src, into(dst), groups, TOP)
        src, dst = dst, src
    sweep(src, finish, rows // 8, FIRST)


def relax(validity, owners, offset, from_a, from_b, image, gx, gy, classes):
    channels, rows, width = image.shape
    tiles = width // LANES
    tall = TOP + rows + 2 * HALO + 8
    smem = pl.BlockSpec(memory_space=pltpu.SMEM)
    hbm = pl.BlockSpec(memory_space=pl.ANY)
    channel = pl.BlockSpec((1, rows, width), lambda k: (k, 0, 0))
    big = pltpu.VMEM((tiles, tall, LANES), f32)
    return pl.pallas_call(
        main_kernel,
        grid=(channels,),
        out_shape=jax.ShapeDtypeStruct(image.shape, f32),
        in_specs=[
            smem, smem, pl.BlockSpec(memory_space=pltpu.VMEM), hbm, hbm,
            channel, channel, channel, pl.BlockSpec((rows, width), lambda k: (0, 0)),
        ],
        out_specs=channel,
        scratch_shapes=[
            pltpu.VMEM((2,) + from_a.shape, bf16),
            big, big, big, big, big, big, big,
            pltpu.VMEM((tall, LANES), f32),
            pltpu.VMEM((tall, LANES), f32),
            pltpu.VMEM((rows + 2 * HALO, LANES), f32),
            pltpu.SemaphoreType.DMA((2,)),
        ],
        name="relax",
    )(validity, owners, offset, from_a, from_b, image, gx, gy, classes)


def pairs_with(offset, devices):
    pairs = []
    for i in range(offset, devices - 1, 2):
        pairs += [(i, i + 1), (i + 1, i)]
    return pairs


def carried_in(sums, channels):
    devices = lax.axis_size("row")
    position = lax.axis_index("row")
    is_total = lax.broadcasted_iota(jnp.int32, sums.shape, 0) < channels
    held, carried = sums, jnp.where(is_total, 0.0, sums)
    by = 1
    while by < devices:
        pairs = [(i, i ^ by) for i in range(devices) if (i ^ by) < devices]
        other = lax.ppermute(held, "row", pairs)
        lower = (position & by) != 0
        carried = carried + jnp.where(is_total & jnp.logical_not(lower), 0.0, other)
        held = held + other
        by *= 2
    return carried


def blended_last_row(gy, owners):
    rows, width = gy.shape[1:]
    devices, position = lax.axis_size("row"), lax.axis_index("row")
    vertical = gy.astype(f32)
    own = lax.dynamic_index_in_dim(owners, position * rows // TILE_ROWS, 0, keepdims=False)
    pairs = [(i, i - 1) for i in range(1, devices)]
    lower = lax.ppermute(jnp.mean(vertical[:, :BAND], axis=1).astype(bf16), "row", pairs)
    upper = jnp.mean(vertical[:, rows - 1 - BAND : rows - 1], axis=1).astype(bf16)
    lower_owns = jnp.repeat(own[:, 0], TILE_COLS, total_repeat_length=width)[None] == 1
    at_seam = (((position + 1) * rows) % TILE_ROWS == 0) & (position < devices - 1)
    last = jnp.where(at_seam, jnp.where(lower_owns, lower, upper), gy[:, -1])
    return gy.at[:, -1].set(last)


def per_device(image, grad_x, grad_y, classes, validity, owners):
    channels, rows, _ = image.shape
    devices = lax.axis_size("row")
    if devices * rows > TILE_ROWS:
        grad_y = blended_last_row(grad_y, owners)
    to_a, to_b, sums = pack(image, grad_x, grad_y, classes)
    from_a = lax.ppermute(to_a, "row", pairs_with(0, devices))
    from_b = lax.ppermute(to_b, "row", pairs_with(1, devices))
    offset = carried_in(sums, channels)
    return relax(validity, owners, offset, from_a, from_b, image, grad_x, grad_y, classes)


def solution(mesh):
    split = ("win", "row")
    in_specs = (
        P(None, split, None), P(None, split, None), P(None, split, None),
        P(split, None), P("win", None), P("win", None, None),
    )
    return jax.shard_map(
        per_device, mesh=mesh, in_specs=in_specs, out_specs=P(None, split, None), check_vma=False
    )
```

time: 212 us -> 57.8 us (0.27); the launches traced: 209 us -> 57.5 us
  other arithmetic: 70.1 us -> 2.02 us
  local copies, waits for them, and re-layouts: 63.3 us -> 2.21 us
  blocking collectives: 35.7 us -> 0 us
  Pallas kernels: 0 us -> 29.5 us
  loops' own time: 9.62 us -> 0 us
  starting transfers between devices: 23.5 us -> 14.9 us
  waiting for transfers between devices: 5.24 us -> 8.77 us
    add x7 -> x4, other arithmetic: 39.7 us -> 2 us  [the longest x1 1.33 us: carried_in(): carried = carried + jnp.where(is_total & jnp.logical_not(lower), 0.0, other)]
    unnamed x1 -> x0, blocking collectives: 35.7 us -> none
    scatter x2 -> x0, local copies, waits for them, and re-layouts: 34.8 us -> none  [the longest x1 34.4 us: per_device(): horiz_tiles.at[:, :, :-1, TILE_COLS - 1]]
    pallas_call x0 -> x2, Pallas kernels: none -> 29.5 us  [the longest x1 25 us: relax(): pl.pallas_call(main_kernel, grid=(channels,), out_shape=jax.ShapeDtypeStr...]
    concatenate x6 -> x0, other arithmetic: 13.3 us -> none  [the longest x4 8.71 us: with_halo(): block = jnp.concatenate([low, block, high], axis=dim)]
    another operation x1 -> x0, loops' own time: 9.62 us -> none  [carried_in(): return lax.fori_loop(0, devices, turn, start)]
    dynamic_slice x16 -> x0, local copies, waits for them, and re-layouts: 9.46 us -> none  [turn(): new = combine(before, jax.tree.map(lambda part: part[k], everything))]
    reshape x2 -> x0, local copies, waits for them, and re-layouts: 9.01 us -> none  [the longest x1 5.1 us: per_device(): horiz_tiles = horizontal.reshape(3, band_rows, TILES_X, TILE_COLS)]
  transfers between devices with their start and end apart: 11 -> 6, of which waited for: 3 -> 4; matrix products, arithmetic and copies ran while one was open for 17% -> 5% of each run, Pallas kernels for 0% -> 0%
where the time goes in v1:
time: 57.8 us; the launch traced here: 57.5 us
  Pallas kernels  29.5 us (51%)
  starting transfers between devices  14.9 us (26%)
  waiting for transfers between devices  8.77 us (15%)
  local copies, waits for them, and re-layouts  2.21 us (4%)
  other arithmetic  2.02 us (3%)
    pallas_call x1, Pallas kernels, relax(): pl.pallas_call(main_kernel, grid=(channels,), out_shape=jax.ShapeDtypeStr...  25 us
    ppermute x4, starting transfers between devices, carried_in(): other = lax.ppermute(held, 'row', pairs)  14.2 us
    ppermute x4, waiting for transfers between devices, carried_in(): other = lax.ppermute(held, 'row', pairs)  8.76 us
    pallas_call x1, Pallas kernels, pack(): pl.pallas_call(pack_kernel, out_shape=(edge, edge, jax.ShapeDtypeStruct((...  4.51 us
    unnamed x7, local copies, waits for them, and re-layouts  2.21 us
    add x1, other arithmetic, carried_in(): carried = carried + jnp.where(is_total & jnp.logical_not(lower), 0.0, other)  1.33 us
  transfers between devices with their start and end apart: 6, of which 4 were waited for; matrix products, arithmetic and copies ran while one was open for 5% of the time, Pallas kernels for 0%

profile of v1, /device:TPU:0, one launch (start us, length us, event | category | flops | bytes accessed | tf_op | source)
XLA Modules:
  0.0 57.5 jit_solution(3937221804237905062)
XLA Ops:
  0.0 0.0 copy-start.2
  0.0 4.5 %pack.1 = (bf16[7,8,4096]{2,1,0:T(8,128)(2,1)}, bf16[7,8,4096]{2,1,0:T(8,128)(2,1)}, f32[8,128]{1,0:T(8,128)}) custom-call(f32[3,64,4096]{2,1,0:T(8,128)} %image.3, bf16[3,64,4096]{2,1,0:T(8,128)(2,1)} %gx.3, bf16[3,64,4096]{2,1,0:T(8,128)(2,1)} %gy.3, s32[64,4096]{1,0:T(8,128)} %classes.3, bf16[3,64,4096]{2,1,0:T(8,128)(2,1)} %gy.3), custom_call_target="tpu_custom_call" | custom-call | tf_op jit(solution)/shard_map/pack/pallas_call | solution.py:112
  4.5 0.6 collective-permute-start
  5.1 0.1 collective-permute-start.4
  5.2 0.7 %collective-permute-start.5 = (bf16[7,8,4096]{2,1,0:T(8,128)(2,1)}, bf16[7,8,4096]{2,1,0:T(8,128)(2,1)S(1)}, u32[]{:S(2)}, u32[]{:S(2)}) collective-permute-start(bf16[7,8,4096]{2,1,0:T(8,128)(2,1)} %get-tuple-element.10), channel_id=1, source_target_pairs={{1,2},{2,1},{3,4},{4,3},{5,6},{6,5},{7,8},{8,7},{9,10},{10,9},{11,... | collective-permute-start | bytes 1376264 | tf_op jit(solution)/shard_map/ppermute | solution.py:418
  5.9 0.3 collective-permute-done
  6.1 0.7 %add.22 = f32[8,128]{1,0:T(8,128)S(1)} add(f32[8,128]{1,0:T(8,128)} %get-tuple-element.8, f32[8,128]{1,0:T(8,128)S(1)} %collective-permute-done) | non-fusion elementwise | flops 1024 | bytes 12288 | tf_op jit(solution)/shard_map/add | solution.py:392
  6.8 3.9 %collective-permute-start.1 = (f32[8,128]{1,0:T(8,128)S(1)}, f32[8,128]{1,0:T(8,128)S(1)}, u32[]{:S(2)}, u32[]{:S(2)}) collective-permute-start(f32[8,128]{1,0:T(8,128)S(1)} %add.22), channel_id=1, source_target_pairs={{0,2},{1,3},{2,0},{3,1},{4,6},{5,7},{6,4},{7,5},{8,10},{9,11},{10,... | collective-permute-start | bytes 12296 | tf_op jit(solution)/shard_map/ppermute | solution.py:389
  10.7 6.0 %collective-permute-done.1 = f32[8,128]{1,0:T(8,128)S(1)} collective-permute-done((f32[8,128]{1,0:T(8,128)S(1)}, f32[8,128]{1,0:T(8,128)S(1)}, u32[]{:S(2)}, u32[]{:S(2)}) %collective-permute-start.1) | collective-permute-done | bytes 4128 | tf_op jit(solution)/shard_map/ppermute | solution.py:389
  16.7 6.7 %collective-permute-start.2 = (f32[8,128]{1,0:T(8,128)S(1)}, f32[8,128]{1,0:T(8,128)S(1)}, u32[]{:S(2)}, u32[]{:S(2)}) collective-permute-start(f32[8,128]{1,0:T(8,128)S(1)} %add.24), channel_id=1, source_target_pairs={{0,4},{1,5},{2,6},{3,7},{4,0},{5,1},{6,2},{7,3},{8,12},{9,13},{10,... | collective-permute-start | bytes 12296 | tf_op jit(solution)/shard_map/ppermute | solution.py:389
  23.4 1.6 %collective-permute-done.2 = f32[8,128]{1,0:T(8,128)S(1)} collective-permute-done((f32[8,128]{1,0:T(8,128)S(1)}, f32[8,128]{1,0:T(8,128)S(1)}, u32[]{:S(2)}, u32[]{:S(2)}) %collective-permute-start.2) | collective-permute-done | bytes 4128 | tf_op jit(solution)/shard_map/ppermute | solution.py:389
  25.0 3.0 %collective-permute-start.3 = (f32[8,128]{1,0:T(8,128)S(1)}, f32[8,128]{1,0:T(8,128)S(1)}, u32[]{:S(2)}, u32[]{:S(2)}) collective-permute-start(f32[8,128]{1,0:T(8,128)S(1)} %add.26), channel_id=1, source_target_pairs={{0,8},{1,9},{2,10},{3,11},{4,12},{5,13},{6,14},{7,15},{8,0},{9,1},... | collective-permute-start | bytes 12296 | tf_op jit(solution)/shard_map/ppermute | solution.py:389
  28.0 0.0 copy-done.2
  28.0 0.7 %copy.7.owners = s32[1,4,2]{2,1,0:T(4,128)} copy(s32[1,4,2]{1,2,0:T(2,128)S(1)} %copy-done.2) | data formatting | bytes 64 | tf_op args[5]
  28.7 0.9 %collective-permute-done.3 = f32[8,128]{1,0:T(8,128)S(1)} collective-permute-done((f32[8,128]{1,0:T(8,128)S(1)}, f32[8,128]{1,0:T(8,128)S(1)}, u32[]{:S(2)}, u32[]{:S(2)}) %collective-permute-start.3) | collective-permute-done | bytes 4128 | tf_op jit(solution)/shard_map/ppermute | solution.py:389
  29.6 1.3 %select_add_fusion.offset = f32[8,128]{1,0:T(8,128)} fusion(f32[8,128]{1,0:T(8,128)S(1)} %collective-permute-done.3, f32[8,128]{1,0:T(8,128)S(1)} %collective-permute-done.2, f32[8,128]{1,0:T(8,128)S(1)} %collective-permute-done.1, f32[8,128]{1,0:T(8,128)S(1)} %collective-permute-done, f32[8,128]{1,0:T(8,128)} %get-tuple-element.8, ...), kind=kLoop, calls=%fused_computation | loop fusion | flops 9216 | bytes 24616 | tf_op jit(solution)/shard_map/add | solution.py:391
  30.9 0.0 collective-permute-done.4.from_a
  31.0 0.0 copy-start
  31.0 0.0 collective-permute-done.5.from_b
  31.0 0.8 %copy-done = bf16[7,8,4096]{2,1,0:T(8,128)(2,1)} copy-done((bf16[7,8,4096]{2,1,0:T(8,128)(2,1)}, bf16[7,8,4096]{2,1,0:T(8,128)(2,1)S(1)}, u32[]{:S(2)}) %copy-start) | copy-done | bytes 458776
  31.7 0.0 copy-start.1
  31.7 0.8 %copy-done.1 = bf16[7,8,4096]{2,1,0:T(8,128)(2,1)} copy-done((bf16[7,8,4096]{2,1,0:T(8,128)(2,1)}, bf16[7,8,4096]{2,1,0:T(8,128)(2,1)S(1)}, u32[]{:S(2)}) %copy-start.1) | copy-done | bytes 458776
  32.5 25.0 %relax.1 = f32[3,64,4096]{2,1,0:T(8,128)} custom-call(s32[1,4]{1,0:T(1,128)} %validity.1, s32[1,4,2]{2,1,0:T(4,128)} %copy.7.owners, f32[8,128]{1,0:T(8,128)} %select_add_fusion.offset, bf16[7,8,4096]{2,1,0:T(8,128)(2,1)} %copy-done, bf16[7,8,4096]{2,1,0:T(8,128)(2,1)} %copy-done.1, f32[3,64,4096]{2,1,0:T(8,128)} %image.3, bf16[3,64,4096]{2,1,0:T(8,128)(2,1)} %gx.3, ...), custom_call_target="tpu_custom_call" | custom-call | tf_op jit(solution)/shard_map/relax/pallas_call | solution.py:353
  (5 shorter events, 0.0 us)
Async XLA Ops:
  0.0 28.0 %copy-start.2 = (s32[1,4,2]{1,2,0:T(2,128)S(1)}, s32[1,4,2]{1,2,0:T(2,128)}, u32[]{:S(2)}) copy-start(s32[1,4,2]{1,2,0:T(2,128)} %param.11) | copy-start | bytes 100
  4.5 1.6 %collective-permute-start = (f32[8,128]{1,0:T(8,128)}, f32[8,128]{1,0:T(8,128)S(1)}, u32[]{:S(2)}, u32[]{:S(2)}) collective-permute-start(f32[8,128]{1,0:T(8,128)} %get-tuple-element.8), channel_id=1, source_target_pairs={{0,1},{1,0},{2,3},{3,2},{4,5},{5,4},{6,7},{7,6},{8,9},{9,8},{10,11... | collective-permute-start | bytes 12296 | tf_op jit(solution)/shard_map/ppermute | solution.py:389
  5.1 25.9 %collective-permute-start.4 = (bf16[7,8,4096]{2,1,0:T(8,128)(2,1)}, bf16[7,8,4096]{2,1,0:T(8,128)(2,1)S(1)}, u32[]{:S(2)}, u32[]{:S(2)}) collective-permute-start(bf16[7,8,4096]{2,1,0:T(8,128)(2,1)} %get-tuple-element.9), channel_id=1, source_target_pairs={{0,1},{1,0},{2,3},{3,2},{4,5},{5,4},{6,7},{7,6},{8,9},{9,8},{10,11... | collective-permute-start | bytes 1376264 | tf_op jit(solution)/shard_map/ppermute | solution.py:417
  5.2 25.8 %collective-permute-start.5 = (bf16[7,8,4096]{2,1,0:T(8,128)(2,1)}, bf16[7,8,4096]{2,1,0:T(8,128)(2,1)S(1)}, u32[]{:S(2)}, u32[]{:S(2)}) collective-permute-start(bf16[7,8,4096]{2,1,0:T(8,128)(2,1)} %get-tuple-element.10), channel_id=1, source_target_pairs={{1,2},{2,1},{3,4},{4,3},{5,6},{6,5},{7,8},{8,7},{9,10},{10,9},{11,... | collective-permute-start | bytes 1376264 | tf_op jit(solution)/shard_map/ppermute | solution.py:418
  6.8 9.9 %collective-permute-start.1 = (f32[8,128]{1,0:T(8,128)S(1)}, f32[8,128]{1,0:T(8,128)S(1)}, u32[]{:S(2)}, u32[]{:S(2)}) collective-permute-start(f32[8,128]{1,0:T(8,128)S(1)} %add.22), channel_id=1, source_target_pairs={{0,2},{1,3},{2,0},{3,1},{4,6},{5,7},{6,4},{7,5},{8,10},{9,11},{10,... | collective-permute-start | bytes 12296 | tf_op jit(solution)/shard_map/ppermute | solution.py:389
  16.7 8.3 %collective-permute-start.2 = (f32[8,128]{1,0:T(8,128)S(1)}, f32[8,128]{1,0:T(8,128)S(1)}, u32[]{:S(2)}, u32[]{:S(2)}) collective-permute-start(f32[8,128]{1,0:T(8,128)S(1)} %add.24), channel_id=1, source_target_pairs={{0,4},{1,5},{2,6},{3,7},{4,0},{5,1},{6,2},{7,3},{8,12},{9,13},{10,... | collective-permute-start | bytes 12296 | tf_op jit(solution)/shard_map/ppermute | solution.py:389
  25.0 4.6 %collective-permute-start.3 = (f32[8,128]{1,0:T(8,128)S(1)}, f32[8,128]{1,0:T(8,128)S(1)}, u32[]{:S(2)}, u32[]{:S(2)}) collective-permute-start(f32[8,128]{1,0:T(8,128)S(1)} %add.26), channel_id=1, source_target_pairs={{0,8},{1,9},{2,10},{3,11},{4,12},{5,13},{6,14},{7,15},{8,0},{9,1},... | collective-permute-start | bytes 12296 | tf_op jit(solution)/shard_map/ppermute | solution.py:389
  31.0 0.8 %copy-start = (bf16[7,8,4096]{2,1,0:T(8,128)(2,1)}, bf16[7,8,4096]{2,1,0:T(8,128)(2,1)S(1)}, u32[]{:S(2)}) copy-start(bf16[7,8,4096]{2,1,0:T(8,128)(2,1)S(1)} %collective-permute-done.4.from_a) | copy-start | bytes 1376260
  31.7 0.8 %copy-start.1 = (bf16[7,8,4096]{2,1,0:T(8,128)(2,1)}, bf16[7,8,4096]{2,1,0:T(8,128)(2,1)S(1)}, u32[]{:S(2)}) copy-start(bf16[7,8,4096]{2,1,0:T(8,128)(2,1)S(1)} %collective-permute-done.5.from_b) | copy-start | bytes 1376260

commit v2 on v1

v2 whole, which is shorter than its diff:
```python
import jax
import jax.numpy as jnp
from jax import lax
from jax.experimental import pallas as pl
from jax.experimental.pallas import tpu as pltpu
from jax.sharding import PartitionSpec as P

TILE_ROWS = 1024
TILE_COLS = 1024
BAND = 48
SWEEPS = 4
OMEGA = 0.8
SCREEN = 0.25

LANES = 128
HALO = SWEEPS
TOP = 8
FIRST = TOP + HALO
SCOPED = 16 << 20
f32 = jnp.float32
bf16 = jnp.bfloat16


def lane_tile(j):
    return slice(j * LANES, (j + 1) * LANES)


def sublane_ids():
    return lax.broadcasted_iota(jnp.int32, (8, LANES), 0)


def lane_ids():
    return lax.broadcasted_iota(jnp.int32, (8, LANES), 1)


def pack_kernel(image, gx, classes, gy, to_a, to_b, sums, img_e, gx_e, cls_e, sem):
    channels, rows, width = image.shape
    tiles = width // LANES
    position = lax.axis_index("row")
    even = position % 2 == 0
    copies = []
    for side, start in enumerate((0, rows - 8)):
        window = pl.ds(start, 8)
        for n, (src, dst) in enumerate(((image, img_e), (gx, gx_e))):
            copies.append(pltpu.make_async_copy(src.at[:, window, :], dst.at[side], sem.at[side, n]))
        copies.append(pltpu.make_async_copy(classes.at[window, :], cls_e.at[side], sem.at[side, 2]))
    for copy in copies:
        copy.start()
    low_half = sublane_ids() < 4
    ones = jnp.ones((8, rows), bf16)
    for k in range(channels):
        total = jnp.zeros((8, LANES), f32)
        for at in range(0, width, 512):
            part = jnp.dot(ones, gy[k, :, at : at + 512], preferred_element_type=f32)
            for i in range(0, 512, LANES):
                total = total + part[:, i : i + LANES]
        total = jnp.sum(total[:1], axis=1, keepdims=True) / width
        sums[k : k + 1, :] = jnp.broadcast_to(total, (1, LANES))
    for copy in copies:
        copy.wait()
    for k in range(channels):
        lead = jnp.zeros((8, LANES), f32)
        for j in range(tiles):
            lead = lead + img_e[0, k, :, lane_tile(j)]
        lead = jnp.sum(lead[0:1, :], axis=1, keepdims=True) / width
        lead = jnp.where(position == 0, lead, 0.0)
        sums[channels + k : channels + k + 1, :] = jnp.broadcast_to(lead, (1, LANES))
    if 2 * channels < 8:
        sums[2 * channels :, :] = jnp.zeros((8 - 2 * channels, LANES), f32)

    def joined(side, first, second):
        if side == 0:
            return jnp.where(low_half, first, pltpu.roll(second, 4, 0))
        return jnp.where(low_half, pltpu.roll(first, 4, 0), second)

    def fill(side, out):
        def one(j):
            at = pl.ds(pl.multiple_of(j * LANES, LANES), LANES)
            for k in range(channels):
                x = img_e[side, k, :, at]
                high = x.astype(bf16).astype(f32)
                out[2 * k, :, at] = joined(side, high, x - high).astype(bf16)
                y = gy[k, pl.ds(side * (rows - 8), 8), at].astype(f32)
                out[2 * k + 1, :, at] = joined(side, gx_e[side, k, :, at].astype(f32), y).astype(bf16)
            c = cls_e[side, :, at].astype(f32)
            out[2 * channels, :, at] = joined(side, c, c).astype(bf16)

        def step(j, carry):
            one(j)
            return carry

        lax.fori_loop(0, tiles, step, 0, unroll=8)

    @pl.when(even)
    def _():
        fill(1, to_a)
        fill(0, to_b)

    @pl.when(jnp.logical_not(even))
    def _():
        fill(0, to_a)
        fill(1, to_b)


def pack(image, gx, gy, classes):
    channels, rows, width = image.shape
    hbm = pl.BlockSpec(memory_space=pl.ANY)
    vmem = pl.BlockSpec(memory_space=pltpu.VMEM)
    edge = pltpu.VMEM((2 * channels + 1, 8, width), bf16)
    return pl.pallas_call(
        pack_kernel,
        out_shape=(edge, edge, pltpu.VMEM((8, LANES), f32)),
        in_specs=[hbm, hbm, hbm, vmem],
        out_specs=[vmem] * 3,
        scratch_shapes=[
            pltpu.VMEM((2, channels, 8, width), f32),
            pltpu.VMEM((2, channels, 8, width), bf16),
            pltpu.VMEM((2, 8, width), jnp.int32),
            pltpu.SemaphoreType.DMA((2, 3)),
        ],
        compiler_params=pltpu.CompilerParams(vmem_limit_bytes=SCOPED),
        name="pack",
    )(image, gx, classes, gy)


def factors(c, cover):
    w = cover * SCREEN * jnp.exp2(c)
    q = OMEGA / (w + 6.0)
    return q, q * w


def mend_column_seams(x_s, at, half, own_right, per_tile, tiles):
    lanes = lane_ids()
    count = 4 if half else 8
    for b in range(tiles // per_tile - 1):
        j = (b + 1) * per_tile - 1
        left = x_s[j, pl.ds(at, 8), :]
        right = x_s[j + 1, pl.ds(at, 8), :]
        in_right = jnp.where(lanes < BAND, right, 0.0)
        in_left = jnp.where((lanes >= LANES - 1 - BAND) & (lanes < LANES - 1), left, 0.0)
        band = jnp.where(own_right[b], in_right, in_left)
        mean = jnp.sum(band, axis=1, keepdims=True) / BAND
        x_s[j, pl.ds(at, count), :] = jnp.where(lanes == LANES - 1, mean, left)[:count]


def constant_terms(at, x_s, y_s, s_s, q_s, qw_of, b_s, tiles):
    lanes = lane_ids()
    first_lane, last_lane = lanes == 0, lanes == LANES - 1
    zero = jnp.zeros((8, LANES), f32)

    def load(j):
        x = x_s[j, pl.ds(at, 8), :]
        xu = x_s[j, pl.ds(at - 1, 8), :]
        y = y_s[j, pl.ds(at, 8), :]
        yu = y_s[j, pl.ds(at - 1, 8), :]
        f = 3.0 * x + xu
        base = f + 2.0 * (y - 2.0 * yu)
        return base, pltpu.roll(y - f, 1, 1), pltpu.roll(y, LANES - 1, 1)

    prev_rot = zero
    cur = load(0)
    for j in range(tiles):
        nxt = load(j + 1) if j + 1 < tiles else (None, None, zero)
        base, rot_l, rot_r = cur
        twice = base + jnp.where(first_lane, prev_rot, rot_l) + jnp.where(last_lane, nxt[2], rot_r)
        q = q_s[j, pl.ds(at, 8), :]
        b_s[j, pl.ds(at, 8), :] = qw_of(j, q) * s_s[j, pl.ds(at, 8), :] - (0.5 * q) * twice
        prev_rot = rot_l
        cur = nxt


def weight_part(j, q):
    return OMEGA - 6.0 * q


def prepare_kernel(validity, owners, image, gx, gy, classes, s_o, b_o, x_o, y_o, q_s, row_y, row_i, level):
    channels, rows, width = image.shape
    tiles = width // LANES
    per_tile = TILE_COLS // LANES
    position = lax.axis_index("row")
    tile_row = position * rows // TILE_ROWS
    covers = [validity[tile_row, b].astype(f32) for b in range(width // TILE_COLS)]
    own_right = [owners[tile_row, 1, b] == 1 for b in range(width // TILE_COLS - 1)]

    def weights(g, carry):
        at = pl.multiple_of(g * 8, 8)
        for j in range(tiles):
            q, _ = factors(classes[pl.ds(at, 8), lane_tile(j)].astype(f32), covers[j // per_tile])
            q_s[j, pl.ds(FIRST + at, 8), :] = q
        return carry

    lax.fori_loop(0, rows // 8, weights, 0)

    r = lax.broadcasted_iota(jnp.int32, (rows, rows), 0)
    c = lax.broadcasted_iota(jnp.int32, (rows, rows), 1)
    above = jnp.where(c < r, 1.0, 0.0)

    def channel(k, carry):
        s_s, b_s, x_s, y_s = s_o.at[k], b_o.at[k], x_o.at[k], y_o.at[k]

        def unpack(g, carry):
            at = pl.multiple_of(g * 16, 16)
            sum_y = jnp.zeros((16, LANES), f32)
            sum_i = jnp.zeros((16, LANES), f32)
            for j in range(tiles):
                here = pl.ds(FIRST + at, 16)
                x_s[j, here, :] = gx[k, pl.ds(at, 16), lane_tile(j)].astype(f32)
                y = gy[k, pl.ds(at, 16), lane_tile(j)].astype(f32)
                y_s[j, here, :] = y
                sum_y = sum_y + y
                sum_i = sum_i + image[k, pl.ds(at, 16), lane_tile(j)]
            row_y[pl.ds(at, 16), :] = sum_y
            row_i[pl.ds(at, 16), :] = sum_i
            return carry

        lax.fori_loop(0, rows // 16, unpack, 0)
        climbed = jnp.dot(above, row_y[...], precision=lax.Precision.HIGHEST, preferred_element_type=f32)
        lv = jnp.sum(climbed - row_i[...], axis=1, keepdims=True) / width
        level[...] = jnp.broadcast_to(lv, (rows, LANES))
        for g in range(rows // 8):
            mend_column_seams(x_s, FIRST + 8 * g, False, own_right, per_tile, tiles)
            lv = level[8 * g : 8 * g + 8, :]
            for j in range(tiles):
                s_s[j, FIRST + 8 * g : FIRST + 8 * g + 8, :] = image[k, 8 * g : 8 * g + 8, lane_tile(j)] + lv
        for g in range((rows + 2 * HALO) // 8 - 2):
            constant_terms(TOP + 8 + 8 * g, x_s, y_s, s_s, q_s, weight_part, b_s, tiles)
        return carry

    lax.fori_loop(0, channels, channel, 0)


def prepare(validity, owners, image, gx, gy, classes):
    channels, rows, width = image.shape
    tiles = width // LANES
    tall = TOP + rows + 2 * HALO + 8
    smem = pl.BlockSpec(memory_space=pltpu.SMEM)
    vmem = pl.BlockSpec(memory_space=pltpu.VMEM)
    big = pltpu.VMEM((channels, tiles, tall, LANES), f32)
    return pl.pallas_call(
        prepare_kernel,
        out_shape=(big, big, big, big, pltpu.VMEM((tiles, tall, LANES), f32)),
        in_specs=[smem, smem, vmem, vmem, vmem, vmem],
        out_specs=[vmem] * 5,
        scratch_shapes=[pltpu.VMEM((rows, LANES), f32)] * 3,
        compiler_params=pltpu.CompilerParams(vmem_limit_bytes=SCOPED),
        name="prepare",
    )(validity, owners, image, gx, gy, classes)


def sweep_kernel(
    validity, owners, offset, sums, from_a, from_b, s_i, b_i, x_i, y_i, q_i,
    out, s_o, b_o, x_o, y_o, q_s, t_s, stage, sem,
):
    channels, tiles, tall, _ = s_o.shape
    rows = tall - 2 * HALO - TOP - 8
    groups = (rows + 2 * HALO) // 8
    per_tile = TILE_COLS // LANES
    position = lax.axis_index("row")
    last = lax.axis_size("row") - 1
    even = position % 2 == 0
    there = (position > 0, position < last)
    beyond = (
        jnp.maximum(position * rows - 1, 0) // TILE_ROWS,
        jnp.minimum((position + 1) * rows, (last + 1) * rows - 1) // TILE_ROWS,
    )
    own_right = [[owners[t, 1, b] == 1 for b in range(tiles // per_tile - 1)] for t in beyond]
    lanes = lane_ids()
    first_lane, last_lane = lanes == 0, lanes == LANES - 1
    upper = sublane_ids() < HALO

    def halo_of(side, n, j):
        one, other = (from_b, from_a) if side == 0 else (from_a, from_b)
        return jnp.where(even, one[n, :, lane_tile(j)], other[n, :, lane_tile(j)])

    ends = (TOP, FIRST + rows)
    for side, at in enumerate(ends):
        for j in range(tiles):
            cover = validity[beyond[side], j // per_tile].astype(f32)
            q, _ = factors(halo_of(side, 2 * channels, j).astype(f32), cover)
            q_s[j, at : at + HALO, :] = jnp.where(there[side], q, 0.0)[:HALO]

    def channel(k, carry):
        s_s, b_s, x_s, y_s = s_o.at[k], b_o.at[k], x_o.at[k], y_o.at[k]
        c = jnp.broadcast_to(offset[pl.ds(k, 1), :] + offset[pl.ds(k + channels, 1), :], (8, LANES))
        total = jnp.broadcast_to(sums[pl.ds(k, 1), :], (8, LANES))

        for side, at in enumerate(ends):
            sum_y = jnp.zeros((8, LANES), f32)
            sum_i = jnp.zeros((8, LANES), f32)
            for j in range(tiles):
                v = halo_of(side, 2 * k, j).astype(f32)
                i = v + pltpu.roll(v, 4, 0)
                s_s[j, at : at + HALO, :] = i[:HALO]
                g = halo_of(side, 2 * k + 1, j).astype(f32)
                y = pltpu.roll(g, 4, 0)
                x_s[j, at : at + HALO, :] = g[:HALO]
                y_s[j, at : at + HALO, :] = y[:HALO]
                sum_y = sum_y + y
                sum_i = sum_i + i
            mean_y = jnp.where(upper, jnp.sum(sum_y, axis=1, keepdims=True) / (tiles * LANES), 0.0)
            mean_i = jnp.sum(sum_i, axis=1, keepdims=True) / (tiles * LANES)
            if side == 0:
                fall = mean_y + pltpu.roll(mean_y, 7, 0)
                lv = -(fall + pltpu.roll(fall, 6, 0)) - mean_i
            else:
                climb = pltpu.roll(mean_y, 1, 0)
                climb = climb + pltpu.roll(climb, 1, 0)
                lv = total + (climb + pltpu.roll(climb, 2, 0)) - mean_i
            for j in range(tiles):
                v = s_s[j, pl.ds(at, 8), :] + lv
                s_s[j, at : at + HALO, :] = jnp.where(there[side], v, -c)[:HALO]
            mend_column_seams(x_s, at, True, own_right[side], per_tile, tiles)

        for side, at in ((0, TOP), (1, TOP + 8 * groups - 8)):
            constant_terms(at, x_s, y_s, s_s, q_s, weight_part, b_s, tiles)
            for j in range(tiles):
                v = b_s[j, ends[side] : ends[side] + HALO, :]
                b_s[j, ends[side] : ends[side] + HALO, :] = jnp.where(there[side], v, -OMEGA * c[:HALO])

        beyond_lane = -2.0 * c

        def sweep(src, at, write):
            def load(j):
                s = src[j, pl.ds(at, 8), :]
                u = src[j, pl.ds(at - 1, 8), :] + src[j, pl.ds(at + 1, 8), :]
                a = s + 0.5 * u
                return s, u, pltpu.roll(a, 1, 1), pltpu.roll(a, LANES - 1, 1)

            prev_rot = beyond_lane
            cur = load(0)
            for j in range(tiles):
                nxt = load(j + 1) if j + 1 < tiles else (None, None, None, beyond_lane)
                s, u, rot_l, rot_r = cur
                n = u + jnp.where(first_lane, prev_rot, rot_l) + jnp.where(last_lane, nxt[3], rot_r)
                write(j, (1.0 - OMEGA) * s + (q_s[j, pl.ds(at, 8), :] * n + b_s[j, pl.ds(at, 8), :]))
                prev_rot = rot_l
                cur = nxt

        src, dst = s_s, t_s
        for _ in range(SWEEPS - 1):
            for g in range(groups):
                at = TOP + 8 * g

                def keep(j, v, at=at, dst=dst):
                    dst[j, at : at + 8, :] = v

                sweep(src, at, keep)
            src, dst = dst, src
        for g in range(rows // 8):

            def finish(j, v, g=g):
                stage[k, 8 * g : 8 * g + 8, lane_tile(j)] = v + c

            sweep(src, FIRST + 8 * g, finish)
        pltpu.make_async_copy(stage.at[k], out.at[k], sem.at[k]).start()
        return carry

    lax.fori_loop(0, channels, channel, 0)
    for k in range(channels):
        pltpu.make_async_copy(stage.at[k], out.at[k], sem.at[k]).wait()


def sweeps(validity, owners, offset, sums, from_a, from_b, parts, out_shape):
    channels, tiles, tall, _ = parts[0].shape
    smem = pl.BlockSpec(memory_space=pltpu.SMEM)
    vmem = pl.BlockSpec(memory_space=pltpu.VMEM)
    parts = [pltpu.with_memory_space_constraint(p, pltpu.VMEM) for p in parts]
    return pl.pallas_call(
        sweep_kernel,
        out_shape=[jax.ShapeDtypeStruct(out_shape, f32)] + [pltpu.VMEM(p.shape, f32) for p in parts],
        in_specs=[smem, smem] + [vmem] * (4 + len(parts)),
        out_specs=[pl.BlockSpec(memory_space=pl.ANY)] + [vmem] * len(parts),
        input_output_aliases={6 + n: 1 + n for n in range(len(parts))},
        scratch_shapes=[
            pltpu.VMEM((tiles, tall, LANES), f32),
            pltpu.VMEM(out_shape, f32),
            pltpu.SemaphoreType.DMA((channels,)),
        ],
        compiler_params=pltpu.CompilerParams(vmem_limit_bytes=SCOPED),
        name="sweeps",
    )(validity, owners, offset, sums, from_a, from_b, *parts)[0]


def pairs_with(offset, devices):
    pairs = []
    for i in range(offset, devices - 1, 2):
        pairs += [(i, i + 1), (i + 1, i)]
    return pairs


def carried_in(sums, channels):
    devices = lax.axis_size("row")
    position = lax.axis_index("row")
    is_total = lax.broadcasted_iota(jnp.int32, sums.shape, 0) < channels
    held, carried = sums, jnp.where(is_total, 0.0, sums)
    by = 1
    while by < devices:
        pairs = [(i, i ^ by) for i in range(devices) if (i ^ by) < devices]
        other = lax.ppermute(held, "row", pairs)
        lower = (position & by) != 0
        carried = carried + jnp.where(is_total & jnp.logical_not(lower), 0.0, other)
        held = held + other
        by *= 2
    return carried


def blended_last_row(gy, owners):
    rows, width = gy.shape[1:]
    devices, position = lax.axis_size("row"), lax.axis_index("row")
    vertical = gy.astype(f32)
    own = lax.dynamic_index_in_dim(owners, position * rows // TILE_ROWS, 0, keepdims=False)
    pairs = [(i, i - 1) for i in range(1, devices)]
    lower = lax.ppermute(jnp.mean(vertical[:, :BAND], axis=1).astype(bf16), "row", pairs)
    upper = jnp.mean(vertical[:, rows - 1 - BAND : rows - 1], axis=1).astype(bf16)
    lower_owns = jnp.repeat(own[:, 0], TILE_COLS, total_repeat_length=width)[None] == 1
    at_seam = (((position + 1) * rows) % TILE_ROWS == 0) & (position < devices - 1)
    last = jnp.where(at_seam, jnp.where(lower_owns, lower, upper), gy[:, -1])
    return gy.at[:, -1].set(last)


def per_device(image, grad_x, grad_y, classes, validity, owners):
    channels, rows, _ = image.shape
    devices = lax.axis_size("row")
    if devices * rows > TILE_ROWS:
        grad_y = blended_last_row(grad_y, owners)
    owners = jnp.transpose(owners, (0, 2, 1))
    to_a, to_b, sums = pack(image, grad_x, grad_y, classes)
    from_a = lax.ppermute(to_a, "row", pairs_with(0, devices))
    from_b = lax.ppermute(to_b, "row", pairs_with(1, devices))
    offset = carried_in(sums, channels)
    parts = prepare(validity, owners, image, grad_x, grad_y, classes)
    return sweeps(validity, owners, offset, sums, from_a, from_b, parts, image.shape)


def solution(mesh):
    split = ("win", "row")
    in_specs = (
        P(None, split, None), P(None, split, None), P(None, split, None),
        P(split, None), P("win", None), P("win", None, None),
    )
    return jax.shard_map(
        per_device, mesh=mesh, in_specs=in_specs, out_specs=P(None, split, None), check_vma=False
    )
```

time: 57.8 us -> 53.2 us (0.920)
  Pallas kernels: 29.5 us -> 19.1 us
  local copies, waits for them, and re-layouts: 2.21 us -> 9.97 us
  other arithmetic: 2.02 us -> 0.11 us
    pallas_call x2 -> x3, Pallas kernels: 29.5 us -> 19.1 us  [the longest x1 11.9 us: sweeps(): pl.pallas_call(sweep_kernel, out_shape=[jax.ShapeDtypeStruct(out_shape, f...]
    unnamed x7 -> x20, local copies, waits for them, and re-layouts: 2.21 us -> 9.97 us
    add x1, other arithmetic: 1.33 us -> 0.08 us  [carried_in(): carried = carried + jnp.where(is_total & jnp.logical_not(lower), 0.0, other)]
    ppermute x1, starting transfers between devices: 0.68 us -> 1.44 us  [per_device(): from_b = lax.ppermute(to_b, 'row', pairs_with(1, devices))]
    add x3, other arithmetic: 0.67 us -> 0.01 us  [carried_in(): held = held + other]
  transfers between devices with their start and end apart: 6 -> 6, of which waited for: 4 -> 2; matrix products, arithmetic and copies ran while one was open for 5% -> 0% of each run, Pallas kernels for 0% -> 9%
where the time goes in v2:
time: 53.2 us; the launch traced here: 52.8 us
  Pallas kernels  19.1 us (36%)
  starting transfers between devices  15.3 us (29%)
  local copies, waits for them, and re-layouts  9.97 us (19%)
  waiting for transfers between devices  8.21 us (15%)
    ppermute x4, starting transfers between devices, carried_in(): other = lax.ppermute(held, 'row', pairs)  13.8 us
    pallas_call x1, Pallas kernels, sweeps(): pl.pallas_call(sweep_kernel, out_shape=[jax.ShapeDtypeStruct(out_shape, f...  11.9 us
    unnamed x20, local copies, waits for them, and re-layouts  9.97 us
    ppermute x4, waiting for transfers between devices, carried_in(): other = lax.ppermute(held, 'row', pairs)  8.2 us
    pallas_call x1, Pallas kernels, prepare(): pl.pallas_call(prepare_kernel, out_shape=(big, big, big, big, pltpu.VMEM(...  4.59 us
    pallas_call x1, Pallas kernels, pack(): pl.pallas_call(pack_kernel, out_shape=(edge, edge, pltpu.VMEM((8, LANES),...  2.64 us
    ppermute x1, starting transfers between devices, per_device(): from_b = lax.ppermute(to_b, 'row', pairs_with(1, devices))  1.44 us
  transfers between devices with their start and end apart: 6, of which 2 were waited for; matrix products, arithmetic and copies ran while one was open for 0% of the time, Pallas kernels for 9%

profile of v2, /device:TPU:0, one launch (start us, length us, event | category | flops | bytes accessed | tf_op | source)
XLA Modules:
  0.0 52.8 jit_solution(2848339545397367500)
XLA Ops:
  0.0 1.9 %copy-done = f32[3,64,4096]{2,1,0:T(8,128)S(1)} copy-done((f32[3,64,4096]{2,1,0:T(8,128)S(1)}, f32[3,64,4096]{2,1,0:T(8,128)}, u32[]{:S(2)}) %copy-start) | copy-done | bytes 3145752
  1.9 1.4 %copy-done.2 = bf16[3,64,4096]{2,1,0:T(8,128)(2,1)S(1)} copy-done((bf16[3,64,4096]{2,1,0:T(8,128)(2,1)S(1)}, bf16[3,64,4096]{2,1,0:T(8,128)(2,1)}, u32[]{:S(2)}) %copy-start.2) | copy-done | bytes 1572888
  3.3 1.4 %copy-done.4 = bf16[3,64,4096]{2,1,0:T(8,128)(2,1)S(1)} copy-done((bf16[3,64,4096]{2,1,0:T(8,128)(2,1)S(1)}, bf16[3,64,4096]{2,1,0:T(8,128)(2,1)}, u32[]{:S(2)}) %copy-start.4) | copy-done | bytes 1572888
  4.7 1.2 %copy-done.6 = s32[64,4096]{1,0:T(8,128)S(1)} copy-done((s32[64,4096]{1,0:T(8,128)S(1)}, s32[64,4096]{1,0:T(8,128)}, u32[]{:S(2)}) %copy-start.6) | copy-done | bytes 1048600
  5.9 2.6 %pack.1 = (bf16[7,8,4096]{2,1,0:T(8,128)(2,1)}, bf16[7,8,4096]{2,1,0:T(8,128)(2,1)}, f32[8,128]{1,0:T(8,128)S(1)}) custom-call(f32[3,64,4096]{2,1,0:T(8,128)S(1)} %copy-done, bf16[3,64,4096]{2,1,0:T(8,128)(2,1)S(1)} %copy-done.2, s32[64,4096]{1,0:T(8,128)S(1)} %copy-done.6, bf16[3,64,4096]{2,1,0:T(8,128)(2,1)S(1)} %copy-done.4), custom_call_target="tpu_custom_call" | custom-call | tf_op jit(solution)/shard_map/pack/pallas_call | solution.py:110
  8.6 0.6 %collective-permute-start = (f32[8,128]{1,0:T(8,128)S(1)}, f32[8,128]{1,0:T(8,128)S(1)}, u32[]{:S(2)}, u32[]{:S(2)}) collective-permute-start(f32[8,128]{1,0:T(8,128)S(1)} %get-tuple-element.14.sums), channel_id=1, source_target_pairs={{0,1},{1,0},{2,3},{3,2},{4,5},{5,4},{6,7},{7,6},{8,9},{9,8},{10,11... | collective-permute-start | bytes 12296 | tf_op jit(solution)/shard_map/ppermute | solution.py:399
  9.1 0.1 collective-permute-start.4
  9.2 1.4 %collective-permute-start.5 = (bf16[7,8,4096]{2,1,0:T(8,128)(2,1)}, bf16[7,8,4096]{2,1,0:T(8,128)(2,1)}, u32[]{:S(2)}, u32[]{:S(2)}) collective-permute-start(bf16[7,8,4096]{2,1,0:T(8,128)(2,1)} %get-tuple-element.16), channel_id=1, source_target_pairs={{1,2},{2,1},{3,4},{4,3},{5,6},{6,5},{7,8},{8,7},{9,10},{10,9},{11,... | collective-permute-start | bytes 1376264 | tf_op jit(solution)/shard_map/ppermute | solution.py:429
  10.7 0.0 collective-permute-done
  10.7 3.5 %collective-permute-start.1 = (f32[8,128]{1,0:T(8,128)S(1)}, f32[8,128]{1,0:T(8,128)S(1)}, u32[]{:S(2)}, u32[]{:S(2)}) collective-permute-start(f32[8,128]{1,0:T(8,128)S(1)} %add.22), channel_id=1, source_target_pairs={{0,2},{1,3},{2,0},{3,1},{4,6},{5,7},{6,4},{7,5},{8,10},{9,11},{10,... | collective-permute-start | bytes 12296 | tf_op jit(solution)/shard_map/ppermute | solution.py:399
  14.2 6.6 %collective-permute-done.1 = f32[8,128]{1,0:T(8,128)S(1)} collective-permute-done((f32[8,128]{1,0:T(8,128)S(1)}, f32[8,128]{1,0:T(8,128)S(1)}, u32[]{:S(2)}, u32[]{:S(2)}) %collective-permute-start.1) | collective-permute-done | bytes 4128 | tf_op jit(solution)/shard_map/ppermute | solution.py:399
  20.8 6.7 %collective-permute-start.2 = (f32[8,128]{1,0:T(8,128)S(1)}, f32[8,128]{1,0:T(8,128)S(1)}, u32[]{:S(2)}, u32[]{:S(2)}) collective-permute-start(f32[8,128]{1,0:T(8,128)S(1)} %add.24), channel_id=1, source_target_pairs={{0,4},{1,5},{2,6},{3,7},{4,0},{5,1},{6,2},{7,3},{8,12},{9,13},{10,... | collective-permute-start | bytes 12296 | tf_op jit(solution)/shard_map/ppermute | solution.py:399
  27.5 1.6 %collective-permute-done.2 = f32[8,128]{1,0:T(8,128)S(1)} collective-permute-done((f32[8,128]{1,0:T(8,128)S(1)}, f32[8,128]{1,0:T(8,128)S(1)}, u32[]{:S(2)}, u32[]{:S(2)}) %collective-permute-start.2) | collective-permute-done | bytes 4128 | tf_op jit(solution)/shard_map/ppermute | solution.py:399
  29.1 3.0 %collective-permute-start.3 = (f32[8,128]{1,0:T(8,128)S(1)}, f32[8,128]{1,0:T(8,128)S(1)}, u32[]{:S(2)}, u32[]{:S(2)}) collective-permute-start(f32[8,128]{1,0:T(8,128)S(1)} %add.26), channel_id=1, source_target_pairs={{0,8},{1,9},{2,10},{3,11},{4,12},{5,13},{6,14},{7,15},{8,0},{9,1},... | collective-permute-start | bytes 12296 | tf_op jit(solution)/shard_map/ppermute | solution.py:399
  32.1 0.0 copy-start.3
  32.1 1.4 %copy-done.3 = bf16[3,64,4096]{2,1,0:T(8,128)(2,1)S(1)} copy-done((bf16[3,64,4096]{2,1,0:T(8,128)(2,1)S(1)}, bf16[3,64,4096]{2,1,0:T(8,128)(2,1)}, u32[]{:S(2)}) %copy-start.3) | copy-done | bytes 1572888
  33.5 1.4 %copy-done.5 = bf16[3,64,4096]{2,1,0:T(8,128)(2,1)S(1)} copy-done((bf16[3,64,4096]{2,1,0:T(8,128)(2,1)S(1)}, bf16[3,64,4096]{2,1,0:T(8,128)(2,1)}, u32[]{:S(2)}) %copy-start.5) | copy-done | bytes 1572888
  34.9 1.2 %copy-done.7 = s32[64,4096]{1,0:T(8,128)S(1)} copy-done((s32[64,4096]{1,0:T(8,128)S(1)}, s32[64,4096]{1,0:T(8,128)}, u32[]{:S(2)}) %copy-start.7) | copy-done | bytes 1048600
  36.2 4.6 %prepare.1 = (f32[3,32,88,128]{3,2,1,0:T(8,128)S(1)}, f32[3,32,88,128]{3,2,1,0:T(8,128)S(1)}, f32[3,32,88,128]{3,2,1,0:T(8,128)S(1)}, f32[3,32,88,128]{3,2,1,0:T(8,128)S(1)}, f32[32,88,128]{2,1,0:T(8,128)S(1)}) custom-call(s32[1,4]{1,0:T(1,128)S(1)} %copy-done.9, s32[1,2,4]{2,1,0:T(2,128)S(1)} %bitcast.1, f32[3,64,4096]{2,1,0:T(8,128)S(1)} %copy-done.1, ...), custom_call_target="tpu_custom_call" | custom-call | tf_op jit(solution)/shard_map/prepare/pallas_call | solution.py:239
  40.8 0.0 collective-permute-done.3
  40.8 0.1 select_add_fusion.offset
  40.9 0.0 collective-permute-done.4.from_a
  40.9 0.0 collective-permute-done.5.from_b
  40.9 11.9 %sweeps.1 = (f32[3,64,4096]{2,1,0:T(8,128)}, f32[3,32,88,128]{3,2,1,0:T(8,128)S(1)}, f32[3,32,88,128]{3,2,1,0:T(8,128)S(1)}, f32[3,32,88,128]{3,2,1,0:T(8,128)S(...) custom-call(s32[1,4]{1,0:T(1,128)S(1)} %copy-done.9, ...), custom_call_target="tpu_custom_call", output_to_operand_aliasing={{1}: (6, {}), {2}: (7, {}), {3}: (8, {}), {4}: (9, {}), {5}... | custom-call | tf_op jit(solution)/shard_map/sweeps/pallas_call | solution.py:368
  (18 shorter events, 0.0 us)
Async XLA Ops:
  0.0 1.9 %copy-start = (f32[3,64,4096]{2,1,0:T(8,128)S(1)}, f32[3,64,4096]{2,1,0:T(8,128)}, u32[]{:S(2)}) copy-start(f32[3,64,4096]{2,1,0:T(8,128)} %image.3) | copy-start | bytes 9437188
  1.9 1.4 %copy-start.2 = (bf16[3,64,4096]{2,1,0:T(8,128)(2,1)S(1)}, bf16[3,64,4096]{2,1,0:T(8,128)(2,1)}, u32[]{:S(2)}) copy-start(bf16[3,64,4096]{2,1,0:T(8,128)(2,1)} %gx.3) | copy-start | bytes 4718596
  3.3 1.4 %copy-start.4 = (bf16[3,64,4096]{2,1,0:T(8,128)(2,1)S(1)}, bf16[3,64,4096]{2,1,0:T(8,128)(2,1)}, u32[]{:S(2)}) copy-start(bf16[3,64,4096]{2,1,0:T(8,128)(2,1)} %gy.3) | copy-start | bytes 4718596
  4.7 1.2 %copy-start.6 = (s32[64,4096]{1,0:T(8,128)S(1)}, s32[64,4096]{1,0:T(8,128)}, u32[]{:S(2)}) copy-start(s32[64,4096]{1,0:T(8,128)} %classes.3) | copy-start | bytes 3145732
  5.9 26.2 %copy-start.1 = (f32[3,64,4096]{2,1,0:T(8,128)S(1)}, f32[3,64,4096]{2,1,0:T(8,128)}, u32[]{:S(2)}) copy-start(f32[3,64,4096]{2,1,0:T(8,128)} %image.3) | copy-start | bytes 9437188
  5.9 26.2 %copy-start.8 = (s32[1,4,2]{1,2,0:T(2,128)S(1)}, s32[1,4,2]{1,2,0:T(2,128)}, u32[]{:S(2)}) copy-start(s32[1,4,2]{1,2,0:T(2,128)} %param.11) | copy-start | bytes 100
  5.9 26.2 %copy-start.9 = (s32[1,4]{1,0:T(1,128)S(1)}, s32[1,4]{1,0:T(1,128)}, u32[]{:S(2)}) copy-start(s32[1,4]{1,0:T(1,128)} %validity.3) | copy-start | bytes 52
  8.6 2.1 %collective-permute-start = (f32[8,128]{1,0:T(8,128)S(1)}, f32[8,128]{1,0:T(8,128)S(1)}, u32[]{:S(2)}, u32[]{:S(2)}) collective-permute-start(f32[8,128]{1,0:T(8,128)S(1)} %get-tuple-element.14.sums), channel_id=1, source_target_pairs={{0,1},{1,0},{2,3},{3,2},{4,5},{5,4},{6,7},{7,6},{8,9},{9,8},{10,11... | collective-permute-start | bytes 12296 | tf_op jit(solution)/shard_map/ppermute | solution.py:399
  9.1 31.7 %collective-permute-start.4 = (bf16[7,8,4096]{2,1,0:T(8,128)(2,1)}, bf16[7,8,4096]{2,1,0:T(8,128)(2,1)}, u32[]{:S(2)}, u32[]{:S(2)}) collective-permute-start(bf16[7,8,4096]{2,1,0:T(8,128)(2,1)} %get-tuple-element.15), channel_id=1, source_target_pairs={{0,1},{1,0},{2,3},{3,2},{4,5},{5,4},{6,7},{7,6},{8,9},{9,8},{10,11... | collective-permute-start | bytes 1376264 | tf_op jit(solution)/shard_map/ppermute | solution.py:428
  9.2 31.6 %collective-permute-start.5 = (bf16[7,8,4096]{2,1,0:T(8,128)(2,1)}, bf16[7,8,4096]{2,1,0:T(8,128)(2,1)}, u32[]{:S(2)}, u32[]{:S(2)}) collective-permute-start(bf16[7,8,4096]{2,1,0:T(8,128)(2,1)} %get-tuple-element.16), channel_id=1, source_target_pairs={{1,2},{2,1},{3,4},{4,3},{5,6},{6,5},{7,8},{8,7},{9,10},{10,9},{11,... | collective-permute-start | bytes 1376264 | tf_op jit(solution)/shard_map/ppermute | solution.py:429
  10.7 10.1 %collective-permute-start.1 = (f32[8,128]{1,0:T(8,128)S(1)}, f32[8,128]{1,0:T(8,128)S(1)}, u32[]{:S(2)}, u32[]{:S(2)}) collective-permute-start(f32[8,128]{1,0:T(8,128)S(1)} %add.22), channel_id=1, source_target_pairs={{0,2},{1,3},{2,0},{3,1},{4,6},{5,7},{6,4},{7,5},{8,10},{9,11},{10,... | collective-permute-start | bytes 12296 | tf_op jit(solution)/shard_map/ppermute | solution.py:399
  20.8 8.3 %collective-permute-start.2 = (f32[8,128]{1,0:T(8,128)S(1)}, f32[8,128]{1,0:T(8,128)S(1)}, u32[]{:S(2)}, u32[]{:S(2)}) collective-permute-start(f32[8,128]{1,0:T(8,128)S(1)} %add.24), channel_id=1, source_target_pairs={{0,4},{1,5},{2,6},{3,7},{4,0},{5,1},{6,2},{7,3},{8,12},{9,13},{10,... | collective-permute-start | bytes 12296 | tf_op jit(solution)/shard_map/ppermute | solution.py:399
  29.1 11.7 %collective-permute-start.3 = (f32[8,128]{1,0:T(8,128)S(1)}, f32[8,128]{1,0:T(8,128)S(1)}, u32[]{:S(2)}, u32[]{:S(2)}) collective-permute-start(f32[8,128]{1,0:T(8,128)S(1)} %add.26), channel_id=1, source_target_pairs={{0,8},{1,9},{2,10},{3,11},{4,12},{5,13},{6,14},{7,15},{8,0},{9,1},... | collective-permute-start | bytes 12296 | tf_op jit(solution)/shard_map/ppermute | solution.py:399
  32.1 1.4 %copy-start.3 = (bf16[3,64,4096]{2,1,0:T(8,128)(2,1)S(1)}, bf16[3,64,4096]{2,1,0:T(8,128)(2,1)}, u32[]{:S(2)}) copy-start(bf16[3,64,4096]{2,1,0:T(8,128)(2,1)} %gx.3) | copy-start | bytes 4718596
  33.5 1.4 %copy-start.5 = (bf16[3,64,4096]{2,1,0:T(8,128)(2,1)S(1)}, bf16[3,64,4096]{2,1,0:T(8,128)(2,1)}, u32[]{:S(2)}) copy-start(bf16[3,64,4096]{2,1,0:T(8,128)(2,1)} %gy.3) | copy-start | bytes 4718596
  34.9 1.2 %copy-start.7 = (s32[64,4096]{1,0:T(8,128)S(1)}, s32[64,4096]{1,0:T(8,128)}, u32[]{:S(2)}) copy-start(s32[64,4096]{1,0:T(8,128)} %classes.3) | copy-start | bytes 3145732
